TPU v7x, 32 devices: a whole 2x2x4 slice. The times are simulated.
32 devices in a mesh: dp: 4 (over z), ctx: 8 (over y, x, core).
Axes of the slice: x: 2, y: 2, z: 4, core: 2. Of those that a mesh axis runs over, the one named last changes fastest.
Arguments:
- block_input: bfloat16 [4, 2, 1152, 768], P('dp', None, 'ctx'), may hold values from -6 to 6
- cotangent: bfloat16 [4, 2, 1152, 768], P('dp', None, 'ctx'), may hold values from -6 to 6
- tie_map: int32 [13], replicated, may hold values from 0 to 1
- seq_lengths: int32 [4, 2, 4], P('dp'), may hold values from 1 to 1140, 1152 in all within a row
- span_place: int32 [4, 2, 8], P('dp'), may hold values from 0 to 7, each once within a row
- first_gain: bfloat16 [2, 768], P(None, ('dp', 'ctx')), may hold values from 0.099609375 to 1.8984375
- first_shift: bfloat16 [2, 768], P(None, ('dp', 'ctx')), may hold values from -3 to 3
- qkv_weight: bfloat16 [2, 768, 2304], P(None, None, ('dp', 'ctx')), may hold values from -0.3125 to 0.3125
- query_bias: bfloat16 [2, 768], P(None, ('dp', 'ctx')), may hold values from -3 to 3
- value_bias: bfloat16 [2, 768], P(None, ('dp', 'ctx')), may hold values from -3 to 3
- out_weight: bfloat16 [2, 768, 768], P(None, None, ('dp', 'ctx')), may hold values from -0.875 to 0.875
- out_bias: bfloat16 [2, 768], P(None, ('dp', 'ctx')), may hold values from -3 to 3
- second_gain: bfloat16 [2, 768], P(None, ('dp', 'ctx')), may hold values from 0.099609375 to 1.8984375
- second_shift: bfloat16 [2, 768], P(None, ('dp', 'ctx')), may hold values from -3 to 3
- up_weight: bfloat16 [2, 768, 3072], P(None, None, ('dp', 'ctx')), may hold values from -0.21875 to 0.21875
- up_bias: bfloat16 [2, 3072], P(None, ('dp', 'ctx')), may hold values from -3 to 3
- down_weight: bfloat16 [2, 3072, 768], P(None, ('dp', 'ctx')), may hold values from -0.109375 to 0.109375
- down_bias: bfloat16 [2, 768], P(None, ('dp', 'ctx')), may hold values from -3 to 3
Outputs:
- block_output: bfloat16 [4, 2, 1152, 768], P('dp', None, 'ctx')
- input_grad: bfloat16 [4, 2, 1152, 768], P('dp', None, 'ctx')
- first_gain_grad: float32 [2, 768], P(None, ('dp', 'ctx'))
- first_shift_grad: float32 [2, 768], P(None, ('dp', 'ctx'))
- qkv_weight_grad: float32 [2, 768, 2304], P(None, None, ('dp', 'ctx'))
- query_bias_grad: float32 [2, 768], P(None, ('dp', 'ctx'))
- value_bias_grad: float32 [2, 768], P(None, ('dp', 'ctx'))
- out_weight_grad: float32 [2, 768, 768], P(None, None, ('dp', 'ctx'))
- out_bias_grad: float32 [2, 768], P(None, ('dp', 'ctx'))
- second_gain_grad: float32 [2, 768], P(None, ('dp', 'ctx'))
- second_shift_grad: float32 [2, 768], P(None, ('dp', 'ctx'))
- up_weight_grad: float32 [2, 768, 3072], P(None, None, ('dp', 'ctx'))
- up_bias_grad: float32 [2, 3072], P(None, ('dp', 'ctx'))
- down_weight_grad: float32 [2, 3072, 768], P(None, ('dp', 'ctx'))
- down_bias_grad: float32 [2, 768], P(None, ('dp', 'ctx'))
Inputs may be any that keep to these rules, and one draw needn't show every extreme that they name: `seq_lengths`: each row of 4 lengths sums to 1152, and its largest is exactly 1140. `span_place`: each row is a permutation of the 8 block numbers.
All inputs are finite; a program needn't handle non-finite values.
Results may differ from a plain program's by a relative error of at most 0.02.
Values may be sent and summed in bfloat16 or wider, within the bound.
A program may use at most 256 MiB of HBM per device.

v0:
```python
import math

import jax
import jax.numpy as jnp
from jax import lax
from jax.sharding import PartitionSpec as P

HEADS = 12
HD = 64


epsilon = 1e-05
masked_score = -1e30
score_scale = 0.125
key_block = 1024


def layer_norm(inputs, norm_gain, norm_shift):
    average = jnp.mean(inputs, axis=-1, keepdims=True)
    centered = inputs - average
    variance = jnp.mean(centered * centered, axis=-1, keepdims=True)
    return centered * lax.rsqrt(variance + epsilon) * norm_gain + norm_shift


def gelu_tanh(inputs):
    return jax.nn.gelu(inputs, approximate=True)


def stream_positions(row_index, span_row, rows_each):
    owner_lane = row_index // rows_each
    lane_ids = jnp.arange(span_row.shape[0], dtype=jnp.int32)
    span_ids = jnp.sum(
        jnp.where(owner_lane[:, None] == lane_ids[None, :], span_row[None, :], 0), axis=1
    )
    return span_ids * rows_each + row_index % rows_each


def segment_ids(positions, seq_ends):
    return jnp.sum((positions[:, None] >= seq_ends[None, :]).astype(jnp.int32), axis=1)


def over_blocks(step_fn, state, pieces):
    piece_rows = pieces[0].shape[0]
    block_rows = math.gcd(piece_rows, key_block)
    stacked = tuple(
        (
            member.reshape((piece_rows // block_rows, block_rows) + member.shape[1:])
            for member in pieces
        )
    )

    def inner_step(running, scan_item):
        block_index, sliced = scan_item
        return (step_fn(running, sliced, block_index * block_rows), None)

    finished, ignored = lax.scan(
        inner_step, state, (jnp.arange(piece_rows // block_rows, dtype=jnp.int32), stacked)
    )
    return finished


def score_probs(
    query_heads,
    grad_heads,
    lse_heads,
    delta_heads,
    query_pos,
    query_seg,
    key_heads,
    value_heads,
    key_pos,
    key_seg,
):
    allowed = (query_seg[:, None] == key_seg[None, :]) & (key_pos[None, :] <= query_pos[:, None])
    scores = (
        jnp.einsum("qhd,khd->hqk", query_heads, key_heads, preferred_element_type=jnp.float32)
        * score_scale
    )
    probs = jnp.where(allowed[None], jnp.exp(scores - lse_heads[:, :, None]), 0.0)
    dprobs = jnp.einsum("qhd,khd->hqk", grad_heads, value_heads, preferred_element_type=jnp.float32)
    dscores = (probs * (dprobs - delta_heads[:, :, None])).astype(jnp.bfloat16)
    return (probs.astype(jnp.bfloat16), dscores)


def on_device(
    block_input,
    cotangent,
    tie_map,
    seq_lengths,
    span_place,
    first_gain,
    first_shift,
    qkv_weight,
    query_bias,
    value_bias,
    out_weight,
    out_bias,
    second_gain,
    second_shift,
    up_weight,
    up_bias,
    down_weight,
    down_bias,
):
    banks = (
        first_gain,
        first_shift,
        qkv_weight,
        query_bias,
        value_bias,
        out_weight,
        out_bias,
        second_gain,
        second_shift,
        up_weight,
        up_bias,
        down_weight,
        down_bias,
    )
    shards = tuple(
        (
            lax.dynamic_index_in_dim(weight_bank, tie_map[bank_number], 0, keepdims=False)
            for bank_number, weight_bank in enumerate(banks)
        )
    )
    micro_count = block_input.shape[1]
    row_count = block_input.shape[2]
    model_width = block_input.shape[3]
    ctx_index = lax.axis_index("ctx")
    local_rows = ctx_index * row_count + jnp.arange(row_count, dtype=jnp.int32)
    totals = None
    outputs = []
    input_grads = []
    for micro_step in range(micro_count):
        params = (
            lax.all_gather(shards[0], ("dp", "ctx"), axis=0, tiled=True),
            lax.all_gather(shards[1], ("dp", "ctx"), axis=0, tiled=True),
            lax.all_gather(shards[2], ("dp", "ctx"), axis=1, tiled=True),
            lax.all_gather(shards[3], ("dp", "ctx"), axis=0, tiled=True),
            lax.all_gather(shards[4], ("dp", "ctx"), axis=0, tiled=True),
            lax.all_gather(shards[5], ("dp", "ctx"), axis=1, tiled=True),
            lax.all_gather(shards[6], ("dp", "ctx"), axis=0, tiled=True),
            lax.all_gather(shards[7], ("dp", "ctx"), axis=0, tiled=True),
            lax.all_gather(shards[8], ("dp", "ctx"), axis=0, tiled=True),
            lax.all_gather(shards[9], ("dp", "ctx"), axis=1, tiled=True),
            lax.all_gather(shards[10], ("dp", "ctx"), axis=0, tiled=True),
            lax.all_gather(shards[11], ("dp", "ctx"), axis=0, tiled=True),
            lax.all_gather(shards[12], ("dp", "ctx"), axis=0, tiled=True),
        )
        (
            gain_before,
            shift_before,
            qkv_full,
            query_add,
            value_add,
            out_full,
            out_add,
            gain_after,
            shift_after,
            up_full,
            up_add,
            down_full,
            down_add,
        ) = params
        span_row = span_place[0, micro_step]
        seq_ends = jnp.cumsum(seq_lengths[0, micro_step])
        query_pos = stream_positions(local_rows, span_row, row_count)
        query_seg = segment_ids(query_pos, seq_ends)
        inputs_wide = block_input[0, micro_step].astype(jnp.float32)
        first_norm = layer_norm(
            inputs_wide, gain_before.astype(jnp.float32), shift_before.astype(jnp.float32)
        ).astype(jnp.bfloat16)
        projected = jnp.dot(first_norm, qkv_full, preferred_element_type=jnp.float32)
        queries = (projected[:, :model_width] + query_add.astype(jnp.float32)).astype(jnp.bfloat16)
        key_rows = projected[:, model_width : 2 * model_width].astype(jnp.bfloat16)
        value_rows = (projected[:, 2 * model_width :] + value_add.astype(jnp.float32)).astype(
            jnp.bfloat16
        )
        query_heads = queries.reshape(row_count, HEADS, HD)
        key_heads_own = key_rows.reshape(row_count, HEADS, HD)
        value_heads_own = value_rows.reshape(row_count, HEADS, HD)

        def attend(state, pieces, offset):
            row_max, row_sum, accumulated = state
            key_part, value_part = pieces
            piece_rows = key_part.shape[0]
            key_pos = stream_positions(
                offset + jnp.arange(piece_rows, dtype=jnp.int32), span_row, row_count
            )
            key_seg = segment_ids(key_pos, seq_ends)
            allowed = (query_seg[:, None] == key_seg[None, :]) & (
                key_pos[None, :] <= query_pos[:, None]
            )
            scores = (
                jnp.einsum(
                    "qhd,khd->hqk",
                    query_heads,
                    key_part.reshape(piece_rows, HEADS, HD),
                    preferred_element_type=jnp.float32,
                )
                * score_scale
            )
            scores = jnp.where(allowed[None], scores, masked_score)
            new_max = jnp.maximum(row_max, jnp.max(scores, axis=2))
            exp_scores = jnp.where(allowed[None], jnp.exp(scores - new_max[:, :, None]), 0.0)
            factor = jnp.exp(row_max - new_max)
            row_sum = row_sum * factor + jnp.sum(exp_scores, axis=2)
            accumulated = accumulated * factor.T[:, :, None] + jnp.einsum(
                "hqk,khd->qhd",
                exp_scores.astype(jnp.bfloat16),
                value_part.reshape(piece_rows, HEADS, HD),
                preferred_element_type=jnp.float32,
            )
            return (new_max, row_sum, accumulated)

        start_state = (
            jnp.full((HEADS, row_count), masked_score, jnp.float32),
            jnp.zeros((HEADS, row_count), jnp.float32),
            jnp.zeros((row_count, HEADS, HD), jnp.float32),
        )
        row_max, row_sum, accumulated = over_blocks(
            attend,
            start_state,
            (
                lax.all_gather(key_rows, "ctx", axis=0, tiled=True),
                lax.all_gather(value_rows, "ctx", axis=0, tiled=True),
            ),
        )
        attended_wide = accumulated / row_sum.T[:, :, None]
        log_sums = row_max + jnp.log(row_sum)
        attended = attended_wide.reshape(row_count, model_width).astype(jnp.bfloat16)
        mixed_out = jnp.dot(
            attended, out_full, preferred_element_type=jnp.float32
        ) + out_add.astype(jnp.float32)
        residual = inputs_wide + mixed_out
        second_norm = layer_norm(
            residual, gain_after.astype(jnp.float32), shift_after.astype(jnp.float32)
        ).astype(jnp.bfloat16)
        up_proj = jnp.dot(second_norm, up_full, preferred_element_type=jnp.float32) + up_add.astype(
            jnp.float32
        )
        activated = gelu_tanh(up_proj).astype(jnp.bfloat16)
        down_proj = jnp.dot(
            activated, down_full, preferred_element_type=jnp.float32
        ) + down_add.astype(jnp.float32)
        outputs.append((residual + down_proj).astype(jnp.bfloat16))
        params = (
            lax.all_gather(shards[0], ("dp", "ctx"), axis=0, tiled=True),
            lax.all_gather(shards[1], ("dp", "ctx"), axis=0, tiled=True),
            lax.all_gather(shards[2], ("dp", "ctx"), axis=1, tiled=True),
            lax.all_gather(shards[3], ("dp", "ctx"), axis=0, tiled=True),
            lax.all_gather(shards[4], ("dp", "ctx"), axis=0, tiled=True),
            lax.all_gather(shards[5], ("dp", "ctx"), axis=1, tiled=True),
            lax.all_gather(shards[6], ("dp", "ctx"), axis=0, tiled=True),
            lax.all_gather(shards[7], ("dp", "ctx"), axis=0, tiled=True),
            lax.all_gather(shards[8], ("dp", "ctx"), axis=0, tiled=True),
            lax.all_gather(shards[9], ("dp", "ctx"), axis=1, tiled=True),
            lax.all_gather(shards[10], ("dp", "ctx"), axis=0, tiled=True),
            lax.all_gather(shards[11], ("dp", "ctx"), axis=0, tiled=True),
            lax.all_gather(shards[12], ("dp", "ctx"), axis=0, tiled=True),
        )
        (
            gain_before,
            shift_before,
            qkv_full,
            query_add,
            value_add,
            out_full,
            out_add,
            gain_after,
            shift_after,
            up_full,
            up_add,
            down_full,
            down_add,
        ) = params
        grad_out = cotangent[0, micro_step].astype(jnp.float32)
        grad_down = grad_out.astype(jnp.bfloat16)
        down_weight_grad = jnp.einsum(
            "rf,rd->fd", activated, grad_down, preferred_element_type=jnp.float32
        )
        down_bias_grad = jnp.sum(grad_down.astype(jnp.float32), axis=0)
        grad_act = jnp.einsum("rd,fd->rf", grad_down, down_full, preferred_element_type=jnp.float32)
        unused_gelu, gelu_back = jax.vjp(gelu_tanh, up_proj)
        grad_up = gelu_back(grad_act)[0].astype(jnp.bfloat16)
        up_weight_grad = jnp.einsum(
            "rd,rf->df", second_norm, grad_up, preferred_element_type=jnp.float32
        )
        up_bias_grad = jnp.sum(grad_up.astype(jnp.float32), axis=0)
        grad_second = jnp.einsum("rf,df->rd", grad_up, up_full, preferred_element_type=jnp.float32)
        unused_second, second_back = jax.vjp(
            layer_norm, residual, gain_after.astype(jnp.float32), shift_after.astype(jnp.float32)
        )
        grad_resid, second_gain_grad, second_shift_grad = second_back(grad_second)
        grad_resid = grad_resid + grad_out
        grad_mixed = grad_resid.astype(jnp.bfloat16)
        out_weight_grad = jnp.einsum(
            "rc,rd->cd", attended, grad_mixed, preferred_element_type=jnp.float32
        )
        out_bias_grad = jnp.sum(grad_mixed.astype(jnp.float32), axis=0)
        grad_attended = jnp.einsum(
            "rd,cd->rc", grad_mixed, out_full, preferred_element_type=jnp.float32
        ).astype(jnp.bfloat16)
        grad_heads = grad_attended.reshape(row_count, HEADS, HD)
        delta_rows = jnp.sum(grad_heads.astype(jnp.float32) * attended_wide, axis=2)
        delta_heads = delta_rows.T
        empty_heads = jnp.zeros((row_count, HEADS, HD), jnp.float32)
        stats_whole = (
            lax.all_gather(log_sums.T, "ctx", axis=0, tiled=True),
            lax.all_gather(delta_rows, "ctx", axis=0, tiled=True),
        )

        def mutual(state, pieces, offset):
            grad_query, grad_key, grad_value = state
            key_part, value_part, query_part, gradout_part = pieces
            piece_rows = key_part.shape[0]
            lse_part = lax.dynamic_slice_in_dim(stats_whole[0], offset, piece_rows, 0)
            delta_part = lax.dynamic_slice_in_dim(stats_whole[1], offset, piece_rows, 0)
            key_pos = stream_positions(
                offset + jnp.arange(piece_rows, dtype=jnp.int32), span_row, row_count
            )
            key_seg = segment_ids(key_pos, seq_ends)
            key_part_heads = key_part.reshape(piece_rows, HEADS, HD)
            value_part_heads = value_part.reshape(piece_rows, HEADS, HD)
            query_part_heads = query_part.reshape(piece_rows, HEADS, HD)
            gradout_heads = gradout_part.reshape(piece_rows, HEADS, HD)
            probs, dscores = score_probs(
                query_heads,
                grad_heads,
                log_sums,
                delta_heads,
                query_pos,
                query_seg,
                key_part_heads,
                value_part_heads,
                key_pos,
                key_seg,
            )
            grad_query = grad_query + score_scale * jnp.einsum(
                "hqk,khd->qhd", dscores, key_part_heads, preferred_element_type=jnp.float32
            )
            probs_other, dscores_other = score_probs(
                query_part_heads,
                gradout_heads,
                lse_part.T,
                delta_part.T,
                key_pos,
                key_seg,
                key_heads_own,
                value_heads_own,
                query_pos,
                query_seg,
            )
            grad_key = grad_key + score_scale * jnp.einsum(
                "hqk,qhd->khd", dscores_other, query_part_heads, preferred_element_type=jnp.float32
            )
            grad_value = grad_value + jnp.einsum(
                "hqk,qhd->khd", probs_other, gradout_heads, preferred_element_type=jnp.float32
            )
            return (grad_query, grad_key, grad_value)

        grad_query, grad_key, grad_value = over_blocks(
            mutual,
            (empty_heads, empty_heads, empty_heads),
            (
                lax.all_gather(key_rows, "ctx", axis=0, tiled=True),
                lax.all_gather(value_rows, "ctx", axis=0, tiled=True),
                lax.all_gather(queries, "ctx", axis=0, tiled=True),
                lax.all_gather(grad_attended, "ctx", axis=0, tiled=True),
            ),
        )
        grad_proj = jnp.concatenate(
            [
                grad_query.reshape(row_count, model_width),
                grad_key.reshape(row_count, model_width),
                grad_value.reshape(row_count, model_width),
            ],
            axis=1,
        ).astype(jnp.bfloat16)
        qkv_weight_grad = jnp.einsum(
            "rc,rp->cp", first_norm, grad_proj, preferred_element_type=jnp.float32
        )
        query_bias_grad = jnp.sum(grad_proj[:, :model_width].astype(jnp.float32), axis=0)
        value_bias_grad = jnp.sum(grad_proj[:, 2 * model_width :].astype(jnp.float32), axis=0)
        grad_first = jnp.einsum(
            "rp,cp->rc", grad_proj, qkv_full, preferred_element_type=jnp.float32
        )
        unused_first, first_back = jax.vjp(
            layer_norm,
            inputs_wide,
            gain_before.astype(jnp.float32),
            shift_before.astype(jnp.float32),
        )
        grad_input, first_gain_grad, first_shift_grad = first_back(grad_first)
        input_grads.append((grad_input + grad_resid).astype(jnp.bfloat16))
        micro_grads = (
            first_gain_grad,
            first_shift_grad,
            qkv_weight_grad,
            query_bias_grad,
            value_bias_grad,
            out_weight_grad,
            out_bias_grad,
            second_gain_grad,
            second_shift_grad,
            up_weight_grad,
            up_bias_grad,
            down_weight_grad,
            down_bias_grad,
        )
        if totals is None:
            totals = micro_grads
        else:
            totals = tuple(
                (left_sum + right_sum for left_sum, right_sum in zip(totals, micro_grads))
            )
    owned = (
        lax.psum_scatter(totals[0], ("dp", "ctx"), scatter_dimension=0, tiled=True),
        lax.psum_scatter(totals[1], ("dp", "ctx"), scatter_dimension=0, tiled=True),
        lax.psum_scatter(totals[2], ("dp", "ctx"), scatter_dimension=1, tiled=True),
        lax.psum_scatter(totals[3], ("dp", "ctx"), scatter_dimension=0, tiled=True),
        lax.psum_scatter(totals[4], ("dp", "ctx"), scatter_dimension=0, tiled=True),
        lax.psum_scatter(totals[5], ("dp", "ctx"), scatter_dimension=1, tiled=True),
        lax.psum_scatter(totals[6], ("dp", "ctx"), scatter_dimension=0, tiled=True),
        lax.psum_scatter(totals[7], ("dp", "ctx"), scatter_dimension=0, tiled=True),
        lax.psum_scatter(totals[8], ("dp", "ctx"), scatter_dimension=0, tiled=True),
        lax.psum_scatter(totals[9], ("dp", "ctx"), scatter_dimension=1, tiled=True),
        lax.psum_scatter(totals[10], ("dp", "ctx"), scatter_dimension=0, tiled=True),
        lax.psum_scatter(totals[11], ("dp", "ctx"), scatter_dimension=0, tiled=True),
        lax.psum_scatter(totals[12], ("dp", "ctx"), scatter_dimension=0, tiled=True),
    )
    bank_grads = tuple(
        (
            lax.dynamic_update_index_in_dim(
                jnp.zeros(weight_bank.shape, jnp.float32), owned_piece, tie_map[bank_number], 0
            )
            for bank_number, (weight_bank, owned_piece) in enumerate(zip(banks, owned))
        )
    )
    block_output = jnp.stack(outputs)[None]
    input_grad = jnp.stack(input_grads)[None]
    return (block_output, input_grad) + bank_grads


def solution(mesh):
    placed = (
        P("dp", None, "ctx", None),
        P("dp", None, "ctx", None),
        P(),
        P("dp", None, None),
        P("dp", None, None),
        P(None, ("dp", "ctx")),
        P(None, ("dp", "ctx")),
        P(None, None, ("dp", "ctx")),
        P(None, ("dp", "ctx")),
        P(None, ("dp", "ctx")),
        P(None, None, ("dp", "ctx")),
        P(None, ("dp", "ctx")),
        P(None, ("dp", "ctx")),
        P(None, ("dp", "ctx")),
        P(None, None, ("dp", "ctx")),
        P(None, ("dp", "ctx")),
        P(None, ("dp", "ctx"), None),
        P(None, ("dp", "ctx")),
    )
    return jax.shard_map(
        on_device,
        mesh=mesh,
        in_specs=placed,
        out_specs=(
            P("dp", None, "ctx", None),
            P("dp", None, "ctx", None),
            P(None, ("dp", "ctx")),
            P(None, ("dp", "ctx")),
            P(None, None, ("dp", "ctx")),
            P(None, ("dp", "ctx")),
            P(None, ("dp", "ctx")),
            P(None, None, ("dp", "ctx")),
            P(None, ("dp", "ctx")),
            P(None, ("dp", "ctx")),
            P(None, ("dp", "ctx")),
            P(None, None, ("dp", "ctx")),
            P(None, ("dp", "ctx")),
            P(None, ("dp", "ctx"), None),
            P(None, ("dp", "ctx")),
        ),
        check_vma=False,
    )
```

profile of v0, /device:TPU:23, one launch (start us, length us, event | category | flops | bytes accessed | tf_op | source)
XLA Modules:
  0.0 1169.4 jit_solution(1087972306172488219)
XLA Ops:
  38.0 40.1 %all-reduce.19 = (bf16[768]{0:T(1024)(128)(2,1)S(1)}, bf16[768]{0:T(1024)(128)(2,1)S(1)}, bf16[768]{0:T(1024)(128)(2,1)S(1)}, bf16[768]{0:T(1024)(128)(2,1)S(1)}...) all-reduce(bf16[768]{0:T(1024)(128)(2,1)S(1)} %dynamic-update-slice, ...), channel_id=3, replica_groups=mesh['dp'=4,'ctx'=8] {'dp','ctx'}, use_global_device_ids=true, to_apply=%add.1 | all-reduce | flops 9216 | bytes 36864
  106.4 5.7 all-gather.34.cloned.1.call-done
  115.9 24.6 %all-gather.36.cloned.1.call-done = bf16[1152,768]{1,0:T(8,128)(2,1)} async-done(((bf16[144,768]{1,0:T(8,128)(2,1)}), bf16[1152,768]{1,0:T(8,128)(2,1)}) %all-gather.36.cloned.1.call-update) | async-done | bytes 1769488 | tf_op jit(solution)/shard_map/all_gather | solution.py:226
  144.9 77.0 %while.69 = (s32[]{:T(128)}, f32[12,144]{1,0:T(8,128)S(1)}, f32[12,144]{1,0:T(8,128)}, f32[144,12,64]{0,2,1:T(8,128)S(1)}, s32[144]{0:T(256)}, /*index=5*/s32[9]...) while((s32[]{:T(128)}, f32[12,144]{1,0:T(8,128)S(1)}, ...), condition=%wide.region_23.24_spmd.clone, body=%wide.region_18.23_spmd.clone.sunk | while | flops 59017860 | bytes 5130101 | solution.py:56
  230.3 23.2 %all-gather.32.cloned.1.call-done = bf16[1152,768]{1,0:T(8,128)(2,1)} async-done(((bf16[144,768]{1,0:T(8,128)(2,1)}), bf16[1152,768]{1,0:T(8,128)(2,1)}) %all-gather.32.cloned.1.call-update) | async-done | bytes 1769488 | tf_op jit(solution)/shard_map/all_gather | solution.py:226
  253.6 3.9 copy.131
  258.0 67.6 %while.68 = (s32[]{:T(128)}, f32[12,144]{1,0:T(8,128)S(1)}, f32[12,144]{1,0:T(8,128)S(1)}, f32[144,12,64]{0,2,1:T(8,128)S(1)}, s32[144]{0:T(256)}, /*index=5*/s3...) while((s32[]{:T(128)}, f32[12,144]{1,0:T(8,128)S(1)}, ...), condition=%wide.region_10.11_spmd.clone, body=%wide.region_5.10_spmd.clone.sunk | while | flops 59017860 | bytes 5130101 | solution.py:56
  328.8 5.4 fusion.91
  337.1 49.3 %all-gather.52.cloned.1.call-done = bf16[1,3072,768]{2,1,0:T(8,128)(2,1)} async-done(((bf16[1,96,768]{2,1,0:T(8,128)(2,1)}), bf16[1,3072,768]{2,1,0:T(8,128)(2,1)}) %all-gather.52.cloned.1.call-update) | async-done | bytes 4718608 | tf_op jit(solution)/shard_map/all_gather | solution.py:147
  386.4 5.8 convert_reduce_fusion.4
  413.4 9.5 all-gather.15
  423.9 8.4 all-gather.16
  433.1 9.4 all-gather.13
  444.5 8.7 all-gather.14
  456.6 155.8 %while.71 = (s32[]{:T(128)}, f32[144,12,64]{0,2,1:T(8,128)}, f32[144,12,64]{0,2,1:T(8,128)}, f32[144,12,64]{0,2,1:T(8,128)}, bf16[9,128,768]{1,2,0:T(8,128)(2,1)...) while((s32[]{:T(128)}, f32[144,12,64]{0,2,1:T(8,128)}, ...), condition=%wide.region_41.42_spmd.clone, body=%wide.region_38.41_spmd.clone.sunk | while | flops 202058240 | bytes 11886247 | solution.py:56
  612.4 139.8 %while.70 = (s32[]{:T(128)}, f32[144,12,64]{0,2,1:T(8,128)S(1)}, f32[144,12,64]{0,2,1:T(8,128)}, f32[144,12,64]{0,2,1:T(8,128)}, bf16[9,128,768]{1,2,0:T(8,128)(...) while((s32[]{:T(128)}, f32[144,12,64]{0,2,1:T(8,128)S(1)}, ...), condition=%wide.region_32.33_spmd.clone, body=%wide.region_29.32_spmd.clone.sunk | while | flops 202058240 | bytes 15369895 | solution.py:56
  758.3 4.1 convolution_add_fusion
  765.4 5.3 convolution_add_fusion.2
  775.0 5.4 convolution_add_fusion.1
  781.2 4.2 fusion.150
  793.0 39.7 %all-reduce.18 = (f32[768]{0:T(1024)S(1)}, f32[768]{0:T(1024)S(1)}, f32[768]{0:T(1024)S(1)}, f32[768]{0:T(1024)S(1)}, f32[768]{0:T(1024)S(1)}, /*index=5*/f32[76...) all-reduce(f32[768]{0:T(1024)S(1)} %add.802, ...), channel_id=15, replica_groups=mesh['dp'=4,'ctx'=8] {'dp','ctx'}, use_global_device_ids=true, to_apply=%region_46.47.clone | all-reduce | flops 9216 | bytes 73728
  836.2 42.9 %reduce-scatter.5.cloned.1.call-done = f32[768,72]{0,1:T(8,128)} async-done(((f32[768,2304]{0,1:T(8,128)}), f32[768,72]{0,1:T(8,128)}) %reduce-scatter.5.cloned.1.call-update) | async-done | bytes 221200 | tf_op jit(solution)/shard_map/reduce_scatter | solution.py:420
  880.1 139.2 %reduce-scatter.9.cloned.1.call-done = f32[768,96]{0,1:T(8,128)} async-done(((f32[768,3072]{0,1:T(8,128)}), f32[768,96]{0,1:T(8,128)}) %reduce-scatter.9.cloned.1.call-update) | async-done | bytes 294928 | tf_op jit(solution)/shard_map/reduce_scatter | solution.py:427
  1020.3 140.3 %reduce-scatter.11.cloned.1.call-done = f32[96,768]{1,0:T(8,128)} async-done(((f32[3072,768]{1,0:T(8,128)}), f32[96,768]{1,0:T(8,128)}) %reduce-scatter.11.cloned.1.call-update) | async-done | bytes 294928 | tf_op jit(solution)/shard_map/reduce_scatter | solution.py:429
  (1082 shorter events, 525.1 us)
Async XLA Ops:
  7.2 88.4 %copy-start = (bf16[2,768,96]{1,2,0:T(8,128)(2,1)S(1)}, bf16[2,768,96]{1,2,0:T(8,128)(2,1)}, u32[]{:S(2)}) copy-start(bf16[2,768,96]{1,2,0:T(8,128)(2,1)} %param.40) | copy-start | bytes 884740
  7.2 73.6 %all-gather.46.cloned.1.call-start = ((), (), s32[]{:S(2)}) async-start(), calls=%async_computation.16 | async-start | bytes 3649536 | tf_op jit(solution)/shard_map/all_gather | solution.py:138
  12.5 99.5 %all-gather.34.cloned.1.call-start = ((), (), s32[]{:S(2)}) async-start(), calls=%async_computation.6 | async-start | bytes 1990656 | tf_op jit(solution)/shard_map/all_gather | solution.py:225
  85.0 55.5 %all-gather.36.cloned.1.call-start = ((), (), s32[]{:S(2)}) async-start(), calls=%async_computation.7 | async-start | bytes 1990656 | tf_op jit(solution)/shard_map/all_gather | solution.py:226
  89.5 133.3 %all-gather.48.cloned.1.call-start = ((), (), s32[]{:S(2)}) async-start(), calls=%async_computation.17 | async-start | bytes 1216512 | tf_op jit(solution)/shard_map/all_gather | solution.py:141
  92.2 134.2 %all-gather.30.cloned.1.call-start = ((), (), s32[]{:S(2)}) async-start(), calls=%async_computation.4 | async-start | bytes 1990656 | tf_op jit(solution)/shard_map/all_gather | solution.py:225
  93.0 160.5 %all-gather.32.cloned.1.call-start = ((), (), s32[]{:S(2)}) async-start(), calls=%async_computation.5 | async-start | bytes 1990656 | tf_op jit(solution)/shard_map/all_gather | solution.py:226
  93.6 235.1 %all-gather.50.cloned.1.call-start = ((), (), s32[]{:S(2)}) async-start(), calls=%async_computation.18 | async-start | bytes 4866048 | tf_op jit(solution)/shard_map/all_gather | solution.py:145
  96.3 290.1 %all-gather.52.cloned.1.call-start = ((), (), s32[]{:S(2)}) async-start(), calls=%async_computation.19 | async-start | bytes 4866048 | tf_op jit(solution)/shard_map/all_gather | solution.py:147
  99.0 357.6 %all-gather.42.cloned.1.call-start = ((), (), s32[]{:S(2)}) async-start(), calls=%async_computation.10 | async-start | bytes 1990656 | tf_op jit(solution)/shard_map/all_gather | solution.py:368
  106.0 350.5 %all-gather.44.cloned.1.call-start = ((), (), s32[]{:S(2)}) async-start(), calls=%async_computation.11 | async-start | bytes 1990656 | tf_op jit(solution)/shard_map/all_gather | solution.py:369
  328.5 72.7 %copy-start.14 = (f32[144,768]{1,0:T(8,128)}, f32[144,768]{1,0:T(8,128)S(1)}, u32[]{:S(2)}) copy-start(f32[144,768]{1,0:T(8,128)S(1)} %get-tuple-element.1652) | copy-start | bytes 1327108
  328.5 72.7 %copy-start.74 = (f32[144]{0:T(256)}, f32[144]{0:T(256)S(1)}, u32[]{:S(2)}) copy-start(f32[144]{0:T(256)S(1)} %broadcast_multiply_fusion.2) | copy-start | bytes 1732
  404.3 208.1 %all-gather.38.cloned.1.call-start = ((), (), s32[]{:S(2)}) async-start(), calls=%async_computation.8 | async-start | bytes 1990656 | tf_op jit(solution)/shard_map/all_gather | solution.py:368
  405.0 207.4 %all-gather.40.cloned.1.call-start = ((), (), s32[]{:S(2)}) async-start(), calls=%async_computation.9 | async-start | bytes 1990656 | tf_op jit(solution)/shard_map/all_gather | solution.py:369
  407.5 427.8 %reduce-scatter.7.cloned.1.call-start = ((), (), s32[]{:S(2)}) async-start(), calls=%async_computation.13 | async-start | bytes 2433024 | tf_op jit(solution)/shard_map/reduce_scatter | solution.py:423
  456.5 422.6 %reduce-scatter.5.cloned.1.call-start = ((), (), s32[]{:S(2)}) async-start(), calls=%async_computation.12 | async-start | bytes 7299072 | tf_op jit(solution)/shard_map/reduce_scatter | solution.py:420
  456.6 155.8 %copy-start.3 = (f32[144,12,64]{0,2,1:T(8,128)S(1)}, f32[144,12,64]{0,2,1:T(8,128)}, u32[]{:S(2)}) copy-start(f32[144,12,64]{0,2,1:T(8,128)} %custom-call.6) | copy-start | bytes 1327108
  762.6 256.7 %reduce-scatter.9.cloned.1.call-start = ((), (), s32[]{:S(2)}) async-start(), calls=%async_computation.14 | async-start | bytes 9732096 | tf_op jit(solution)/shard_map/reduce_scatter | solution.py:427
  770.7 389.9 %reduce-scatter.11.cloned.1.call-start = ((), (), s32[]{:S(2)}) async-start(), calls=%async_computation.15 | async-start | bytes 9732096 | tf_op jit(solution)/shard_map/reduce_scatter | solution.py:429
  834.3 328.2 %copy-start.1 = (bf16[2,768,96]{1,2,0:T(8,128)(2,1)S(1)}, bf16[2,768,96]{1,2,0:T(8,128)(2,1)}, u32[]{:S(2)}) copy-start(bf16[2,768,96]{1,2,0:T(8,128)(2,1)} %param.40) | copy-start | bytes 884740
  836.2 325.5 %copy-start.66 = (f32[2,768,24]{1,2,0:T(8,128)}, f32[2,768,24]{1,2,0:T(8,128)S(1)}, u32[]{:S(2)}) copy-start(f32[2,768,24]{1,2,0:T(8,128)S(1)} %bitcast_dynamic-update-slice_fusion.3) | copy-start | bytes 442372
  880.1 281.7 %copy-start.63 = (f32[2,768,72]{1,2,0:T(8,128)}, f32[2,768,72]{1,2,0:T(8,128)S(1)}, u32[]{:S(2)}) copy-start(f32[2,768,72]{1,2,0:T(8,128)S(1)} %bitcast_dynamic-update-slice_fusion.2) | copy-start | bytes 1327108
  1020.3 141.4 %copy-start.62 = (f32[2,768,96]{1,2,0:T(8,128)}, f32[2,768,96]{1,2,0:T(8,128)S(1)}, u32[]{:S(2)}) copy-start(f32[2,768,96]{1,2,0:T(8,128)S(1)} %bitcast_dynamic-update-slice_fusion.1) | copy-start | bytes 1769476
  (148 other events, 850.5 us)
Sparse Core Ops, SparseCore 0:
  12.6 59.6 all-gather.45
  85.2 26.8 all-gather.33
  114.0 26.5 all-gather.35
  143.9 53.3 all-gather.47
  199.0 26.2 all-gather.29
  227.0 26.5 all-gather.31
  257.0 63.3 all-gather.49
  323.9 62.4 all-gather.51
  388.3 25.5 all-gather.41
  415.7 27.0 all-gather.43
  444.7 26.6 all-gather.37
  473.1 26.5 all-gather.39
  504.9 96.9 reduce-scatter.6
  762.6 116.3 reduce-scatter.4
  884.8 134.4 reduce-scatter.8
  1026.0 134.5 reduce-scatter.10
where the time goes:
time: 1190 us; the launch traced here: 1170 us
  waiting for transfers between devices  427 us (36%)
  matrix products  249 us (21%)
  local copies, waits for them, and re-layouts  165 us (14%)
  other arithmetic  143 us (12%)
  blocking collectives  116 us (10%)
  between operations  41.4 us (3%)
  loops' own time  27.3 us (2%)
    reduce_scatter x1, waiting for transfers between devices, on_device(): lax.psum_scatter(totals[11], ('dp', 'ctx'), scatter_dimension=0, tiled=True)  140 us
    reduce_scatter x1, waiting for transfers between devices, on_device(): lax.psum_scatter(totals[9], ('dp', 'ctx'), scatter_dimension=1, tiled=True)  139 us
    dynamic_slice x126, local copies, waits for them, and re-layouts, over_blocks(): lax.scan(inner_step, state, (jnp.arange(piece_rows // block_rows, dtype=j...  97.9 us
    unnamed x2, blocking collectives  79.9 us
    all_gather x1, waiting for transfers between devices, on_device(): lax.all_gather(shards[11], ('dp', 'ctx'), axis=0, tiled=True)  49.3 us
    all_gather x2, waiting for transfers between devices, on_device(): lax.all_gather(value_rows, 'ctx', axis=0, tiled=True)  47.9 us
    dot_general x18, matrix products, mutual(): jnp.einsum('hqk,qhd->khd', probs_other, gradout_heads, preferred_element_...  44.5 us
    reduce_scatter x1, waiting for transfers between devices, on_device(): lax.psum_scatter(totals[2], ('dp', 'ctx'), scatter_dimension=1, tiled=True)  42.9 us
  transfers between devices with their start and end apart: 16, of which 7 were waited for; matrix products, arithmetic and copies ran while one was open for 46% of the time, Pallas kernels for 0%

commit v1 on v0

--- a/solution.py
+++ b/solution.py
@@ -1,8 +1,11 @@
+import functools
 import math
 
 import jax
 import jax.numpy as jnp
 from jax import lax
+from jax.experimental import pallas as pl
+from jax.experimental.pallas import tpu as pltpu
 from jax.sharding import PartitionSpec as P
 
 HEADS = 12
@@ -82,7 +85,7 @@
     return (probs.astype(jnp.bfloat16), dscores)
 
 
-def on_device(
+def general_plan(
     block_input,
     cotangent,
     tie_map,
@@ -442,47 +445,1431 @@
     return (block_output, input_grad) + bank_grads
 
 
+BF = jnp.bfloat16
+F32 = jnp.float32
+MESH = pl.DeviceIdType.MESH
+ANY = pl.ANY
+SMALL = 8
+VMEM_BYTES = 60 * 2**20
+
+
+def params(collective_id=None):
+    if collective_id is None:
+        return pltpu.CompilerParams(vmem_limit_bytes=VMEM_BYTES)
+    return pltpu.CompilerParams(
+        vmem_limit_bytes=VMEM_BYTES, collective_id=collective_id, has_side_effects=True
+    )
+
+
+def vmem():
+    return pl.BlockSpec(memory_space=pltpu.VMEM)
+
+
+def smem():
+    return pl.BlockSpec(memory_space=pltpu.SMEM)
+
+
+def anywhere():
+    return pl.BlockSpec(memory_space=ANY)
+
+
+def shape(dims, dtype):
+    return jax.ShapeDtypeStruct(dims, dtype)
+
+
+def nn(left, right):
+    return lax.dot_general(left, right, (((1,), (0,)), ((), ())), preferred_element_type=F32)
+
+
+def nt(left, right):
+    return lax.dot_general(left, right, (((1,), (1,)), ((), ())), preferred_element_type=F32)
+
+
+def tn(left, right):
+    return lax.dot_general(left, right, (((0,), (0,)), ((), ())), preferred_element_type=F32)
+
+
+def iota(dims, axis):
+    return lax.broadcasted_iota(jnp.int32, dims, axis)
+
+
+class Place:
+    def __init__(self, depth):
+        self.depth = depth
+        self.z = lax.axis_index("dp")
+        self.r = lax.axis_index("ctx")
+        self.core = self.r % 2
+        self.j = self.r // 2
+        self.a = self.r // 4
+        self.b = (self.r // 2) % 2
+        self.by_a = (1 - self.a) * 4 + self.b * 2 + self.core
+        self.by_b = self.a * 4 + (1 - self.b) * 2 + self.core
+        self.both = (1 - self.a) * 4 + (1 - self.b) * 2 + self.core
+        self.mate = self.j * 2 + 1 - self.core
+
+    def slot(self, z, r):
+        return z * 8 + r
+
+
+def greet(here, whole_plane, line, axes=True):
+    bar = pltpu.get_barrier_semaphore()
+    count = 0
+    if whole_plane:
+        for k in range(1, 8):
+            pl.semaphore_signal(
+                bar, inc=1, device_id=(here.z, (here.r + k) % 8), device_id_type=MESH
+            )
+        count = 7
+    if line:
+        for k in range(1, here.depth):
+            pl.semaphore_signal(
+                bar, inc=1, device_id=((here.z + k) % here.depth, here.r), device_id_type=MESH
+            )
+        count = count + here.depth - 1
+    pl.semaphore_wait(bar, count)
+
+
+def greet_all(here):
+    bar = pltpu.get_barrier_semaphore()
+    total = here.depth * 8
+    me = here.z * 8 + here.r
+
+    def signal(k, carry):
+        other = (me + k) % total
+        pl.semaphore_signal(bar, inc=1, device_id=(other // 8, other % 8), device_id_type=MESH)
+        return carry
+
+    lax.fori_loop(1, total, signal, 0)
+    pl.semaphore_wait(bar, total - 1)
+
+
+def remote(source, target, send, recv, z, r):
+    return pltpu.make_async_remote_copy(
+        src_ref=source,
+        dst_ref=target,
+        send_sem=send,
+        recv_sem=recv,
+        device_id=(z, r),
+        device_id_type=MESH,
+    )
+
+
+def pack_kernel(tie, g1, s1, wq, bq, bv, wo, bo, g2, s2, wu, bu, wd, bd, f_out, q_out):
+    width = wq.shape[1]
+    unit = g1.shape[1]
+    hidden = wu.shape[2]
+
+    def turned(bank, index):
+        return bank[tie[index]].astype(F32).T.astype(BF)
+
+    f_out[0:hidden, :] = turned(wu, 9)
+    f_out[hidden : 2 * hidden, :] = wd[tie[11]]
+    f_out[2 * hidden : 2 * hidden + unit, :] = turned(wo, 5)
+    q_out[...] = turned(wq, 2)
+    f_out[2 * hidden + unit :, :] = jnp.zeros((SMALL, width), BF)
+    base = 2 * hidden + unit
+    banks = ((g1, 0), (s1, 1), (bq, 3), (bv, 4), (bo, 6), (g2, 7), (s2, 8), (bd, 12))
+    rows = []
+    for bank, index in banks:
+        both = bank[...].astype(F32)
+        chosen = jnp.zeros((1, unit), F32)
+        for layer in range(bank.shape[0]):
+            chosen = jnp.where(tie[index] == layer, both[layer : layer + 1, :], chosen)
+        rows.append(chosen)
+    f_out[base : base + SMALL, 0:unit] = jnp.concatenate(rows, axis=0).astype(BF)
+    both = bu[...].astype(F32)
+    chosen = jnp.zeros((1, hidden), F32)
+    for layer in range(bu.shape[0]):
+        chosen = jnp.where(tie[10] == layer, both[layer : layer + 1, :], chosen)
+    tall = jnp.concatenate([chosen, jnp.zeros((SMALL - 1, hidden), F32)], axis=0)
+    f_out[base : base + SMALL, 128 : 128 + hidden] = tall.astype(BF)
+
+
+def pack(tie_map, banks):
+    width = banks[2].shape[1]
+    unit = banks[0].shape[1]
+    hidden = banks[9].shape[2]
+    packed_rows = 2 * hidden + unit + SMALL
+    return pl.pallas_call(
+        pack_kernel,
+        name="pack",
+        out_shape=(shape((packed_rows, width), BF), shape((banks[2].shape[2], width), BF)),
+        in_specs=[smem()] + [vmem()] * 13,
+        out_specs=(vmem(), vmem()),
+        compiler_params=params(),
+    )(tie_map, *banks)
+
+
+def gather_kernel(
+    depth,
+    pieces,
+    q_in,
+    f_in,
+    x_in,
+    q_all,
+    f_all,
+    x_all,
+    zsend,
+    zrecv,
+    send1,
+    recv1,
+    send2,
+    recv2,
+    csend,
+    crecv,
+    xsend,
+    xrecv,
+    own_sem,
+):
+    here = Place(depth)
+    z, r = here.z, here.r
+    ins, alls = (q_in, f_in), (q_all, f_all)
+    greet(here, True, True)
+
+    def move(p, zz, rr, own, send, recv, to_z, to_r):
+        which, start, rows, _ = pieces[p]
+        target = alls[which].at[here.slot(zz, rr), pl.ds(start, rows)]
+        source = ins[which].at[pl.ds(start, rows)] if own else target
+        return remote(source, target, send, recv, to_z, to_r)
+
+    def first(p):
+        return here.by_b if pieces[p][3] == "b" else here.by_a
+
+    def second(p):
+        return here.by_a if pieces[p][3] == "b" else here.by_b
+
+    count = len(pieces)
+    every = range(count)
+
+    for k in range(1, 8):
+        to = (r + k) % 8
+        remote(x_in.at[to % 2], x_all.at[r], xsend.at[to], xrecv.at[r], z, to).start()
+    own_x = pltpu.make_async_copy(x_in.at[here.core], x_all.at[r], own_sem.at[0])
+    own_x.start()
+    own_q = pltpu.make_async_copy(q_in, q_all.at[here.slot(z, r)], own_sem.at[1])
+    own_q.start()
+    own_f = pltpu.make_async_copy(f_in, f_all.at[here.slot(z, r)], own_sem.at[2])
+    own_f.start()
+
+    def up(p, o, own=False):
+        return move(p, o, r, own, zsend.at[p, o, 0], zrecv.at[p, o], z + 1, r)
+
+    def down(p, o, own=False):
+        return move(p, o, r, own, zsend.at[p, o, 1], zrecv.at[p, o], z - 1, r)
+
+    def one(p, o, own=False):
+        return move(p, o, r, own, send1.at[p, o], recv1.at[p, o], z, first(p))
+
+    def two(p, o, rr, lane, own=False):
+        return move(p, o, rr, own, send2.at[p, o, lane], recv2.at[p, o, lane], z, second(p))
+
+    def across(p, o, rr, lane, own=False):
+        return move(p, o, rr, own, csend.at[p, o, lane], crecv.at[p, o, lane], z, here.mate)
+
+    for p in every:
+
+        @pl.when(z + 1 < depth)
+        def _():
+            up(p, z, True).start()
+
+        @pl.when(z > 0)
+        def _():
+            down(p, z, True).start()
+
+        one(p, z, True).start()
+        two(p, z, r, 0, True).start()
+        across(p, z, r, 0, True).start()
+
+    def spread_first(o):
+        for p in every:
+            one(p, o).wait_recv()
+            two(p, o, first(p), 1).start()
+            across(p, o, first(p), 1).start()
+
+    def spread_line(o, below):
+        for p in every:
+            up(p, o).wait_recv()
+            if below:
+
+                @pl.when(z + 1 < depth)
+                def _():
+                    up(p, o).start()
+
+            else:
+
+                @pl.when(z > 0)
+                def _():
+                    down(p, o).start()
+
+            one(p, o).start()
+            two(p, o, r, 0).start()
+            across(p, o, r, 0).start()
+
+    def both_ways(distance, act):
+        @pl.when(z - distance >= 0)
+        def _():
+            act(z - distance, True)
+
+        @pl.when(z + distance < depth)
+        def _():
+            act(z + distance, False)
+
+    for distance in range(1, depth):
+        both_ways(distance, spread_line)
+        if distance == 1:
+            spread_first(z)
+        else:
+            both_ways(distance - 1, lambda o, below: spread_first(o))
+    both_ways(depth - 1, lambda o, below: spread_first(o))
+
+    def spread_second(o):
+        for p in every:
+            two(p, o, second(p), 0).wait_recv()
+            across(p, o, second(p), 2).start()
+            two(p, o, here.both, 1).wait_recv()
+            across(p, o, here.both, 3).start()
+
+    spread_second(z)
+    for distance in range(1, depth):
+        both_ways(distance, lambda o, below: spread_second(o))
+
+    mates = lambda p: (here.mate,)
+    for o in range(depth):
+        for p in every:
+            for lane in range(4):
+                across(p, o, r, lane).wait_recv()
+    for k in range(1, 8):
+        frm = (r + k) % 8
+        remote(x_in.at[0], x_all.at[frm], xsend.at[frm], xrecv.at[frm], z, frm).wait()
+    own_x.wait()
+    own_q.wait()
+    own_f.wait()
+    for p in every:
+        for o in range(depth):
+            one(p, o).wait_send()
+            for lane in range(2):
+                two(p, o, r, lane).wait_send()
+            for lane in range(4):
+                across(p, o, r, lane).wait_send()
+
+            @pl.when((o <= z) & (z + 1 < depth))
+            def _():
+                up(p, o).wait_send()
+
+            @pl.when((o >= z) & (z > 0))
+            def _():
+                down(p, o).wait_send()
+
+
+def gather(depth, q_own, f_own, rows):
+    q_rows, width = q_own.shape
+    f_rows = f_own.shape[0]
+    q_cut = (q_rows // 2 + 7) // 8 * 8
+    f_cut = (f_rows // 2 + 7) // 8 * 8
+    pieces = (
+        (0, 0, q_cut, "b"),
+        (0, q_cut, q_rows - q_cut, "a"),
+        (1, 0, f_cut, "b"),
+        (1, f_cut, f_rows - f_cut, "a"),
+    )
+    n = len(pieces)
+    dma = pltpu.SemaphoreType.DMA
+    total = depth * 8
+    return pl.pallas_call(
+        functools.partial(gather_kernel, depth, pieces),
+        name="gather",
+        out_shape=(
+            shape((total, q_rows, width), BF),
+            shape((total, f_rows, width), BF),
+            shape((8,) + rows.shape[1:], BF),
+        ),
+        in_specs=[anywhere()] * 3,
+        out_specs=(anywhere(),) * 3,
+        scratch_shapes=[
+            dma((n, depth, 2)),
+            dma((n, depth)),
+            dma((n, depth)),
+            dma((n, depth)),
+            dma((n, depth, 2)),
+            dma((n, depth, 2)),
+            dma((n, depth, 4)),
+            dma((n, depth, 4)),
+            dma((8,)),
+            dma((8,)),
+            dma((3,)),
+        ],
+        compiler_params=params(1),
+    )(q_own, f_own, rows)
+
+
+def exchange_kernel(depth, block, out, send, recv, own):
+    here = Place(depth)
+    z, r = here.z, here.r
+    greet(here, True, False)
+    mine = pltpu.make_async_copy(block.at[r], out.at[r], own)
+    mine.start()
+    for k in range(1, 8):
+        to = (r + k) % 8
+        remote(block.at[to], out.at[r], send.at[to], recv.at[r], z, to).start()
+    for k in range(1, 8):
+        frm = (r + k) % 8
+        remote(block.at[frm], out.at[frm], send.at[frm], recv.at[frm], z, frm).wait()
+    mine.wait()
+
+
+def exchange(depth, blocks, collective_id):
+    dma = pltpu.SemaphoreType.DMA
+    return pl.pallas_call(
+        functools.partial(exchange_kernel, depth),
+        name="exchange",
+        out_shape=shape(blocks.shape, blocks.dtype),
+        in_specs=[vmem()],
+        out_specs=vmem(),
+        scratch_shapes=[dma((8,)), dma((8,)), dma],
+        compiler_params=params(collective_id),
+    )(blocks)
+
+
+def spread_units(small, width, hidden_total):
+    devices = small.shape[0]
+    unit = width // devices
+    per = hidden_total // devices
+    flat = small.reshape(devices * SMALL, width)
+    lane = iota((128, width), 1)
+    pick = (lane % unit == iota((128, width), 0)).astype(F32).astype(BF)
+    tall = nn(flat[:, 0:128], pick)
+    row = iota((devices * SMALL, width), 0)
+    col = iota((devices * SMALL, width), 1)
+    tall = jnp.where(col // unit == row // SMALL, tall, 0.0)
+    vectors = jnp.sum(tall.reshape(devices, SMALL, width), axis=0)
+    chosen = (
+        iota((devices, devices * SMALL), 1) == iota((devices, devices * SMALL), 0) * SMALL
+    ).astype(F32).astype(BF)
+    firsts = nn(chosen, flat[:, 128:256]).astype(BF)
+    lane = iota((128, hidden_total), 1)
+    pick = (lane % per == iota((128, hidden_total), 0)).astype(F32).astype(BF)
+    wide = nn(firsts, pick)
+    keep = iota((devices, hidden_total), 1) // per == iota((devices, hidden_total), 0)
+    return vectors, jnp.sum(jnp.where(keep, wide, 0.0), axis=0, keepdims=True)
+
+
+def gather_units(vectors, hidden_row, devices):
+    width = vectors.shape[1]
+    hidden_total = hidden_row.shape[1]
+    unit = width // devices
+    per = hidden_total // devices
+    tall = jnp.broadcast_to(vectors[None], (devices, SMALL, width)).reshape(devices * SMALL, width)
+    row = iota((devices * SMALL, width), 0)
+    col = iota((devices * SMALL, width), 1)
+    tall = jnp.where(col // unit == row // SMALL, tall, 0.0).astype(BF)
+    pick = (iota((width, 128), 0) % unit == iota((width, 128), 1)).astype(F32).astype(BF)
+    left = nn(tall, pick)
+    wide = jnp.broadcast_to(hidden_row, (devices, hidden_total))
+    keep = iota((devices, hidden_total), 1) // per == iota((devices, hidden_total), 0)
+    wide = jnp.where(keep, wide, 0.0).astype(BF)
+    pick = (iota((hidden_total, 128), 0) % per == iota((hidden_total, 128), 1)).astype(F32)
+    firsts = nn(wide, pick.astype(BF)).astype(BF)
+    chosen = (
+        iota((devices * SMALL, devices), 0) == iota((devices * SMALL, devices), 1) * SMALL
+    ).astype(F32).astype(BF)
+    right = nn(chosen, firsts)
+    return (
+        left.astype(BF).reshape(devices, SMALL, 128),
+        right.astype(BF).reshape(devices, SMALL, 128),
+    )
+
+
+def group_slice(row, j, groups):
+    width = row.shape[1] // groups
+    out = jnp.zeros((1, width), F32)
+    for g in range(groups):
+        out = jnp.where(j == g, row[:, g * width : (g + 1) * width], out)
+    return out
+
+
+def group_spread(part, j, groups):
+    return jnp.concatenate([jnp.where(j == g, part, 0.0) for g in range(groups)], axis=1)
+
+
+def block_at(place_ref, micro, position, blocks):
+    found = jnp.int32(0)
+    for s in range(blocks):
+        found = jnp.where(place_ref[0, micro, s] == position, s, found)
+    return found
+
+
+def stack_heads(rows, heads):
+    lane = iota(rows.shape, 1) // HD
+    zero = jnp.zeros_like(rows)
+    return jnp.concatenate([jnp.where(lane == h, rows, zero) for h in range(heads)], axis=0)
+
+
+def unstack_heads(tall, heads):
+    rows = tall.shape[0] // heads
+    lane = iota((rows, tall.shape[1]), 1) // HD
+    out = tall[0:rows]
+    for h in range(1, heads):
+        out = jnp.where(lane == h, tall[h * rows : (h + 1) * rows], out)
+    return out
+
+
+def visible_bias(lens, micro, start, rows, key_start, keys):
+    query = start + iota((rows, 1), 0)
+    begin = jnp.zeros((rows, 1), jnp.int32)
+    end = jnp.int32(0)
+    for s in range(lens.shape[2]):
+        end = end + lens[0, micro, s]
+        begin = jnp.where(query >= end, end, begin)
+    key = key_start + iota((rows, keys), 1)
+    return jnp.where((key >= begin) & (key <= query), 0.0, masked_score)
+
+
+def row_norm(wide):
+    average = jnp.mean(wide, axis=-1, keepdims=True)
+    centered = wide - average
+    variance = jnp.mean(centered * centered, axis=-1, keepdims=True)
+    scale = lax.rsqrt(variance + epsilon)
+    return centered * scale, scale
+
+
+def norm_back(grad, unit, scale):
+    first = jnp.mean(grad, axis=-1, keepdims=True)
+    second = jnp.mean(grad * unit, axis=-1, keepdims=True)
+    return (grad - first - unit * second) * scale
+
+
+QROWS = 128
+KCOLS = 384
+
+
+def forward_kernel(
+    depth,
+    lens,
+    spans,
+    x_all,
+    small,
+    q_all,
+    ao,
+    q_out,
+    k_out,
+    v_out,
+    h_out,
+    u_out,
+    o_out,
+    lse_out,
+    vec_out,
+    hid_out,
+    weights,
+    sems,
+):
+    here = Place(depth)
+    micro = here.core
+    blocks, rows, width = x_all.shape
+    group = weights.shape[1]
+    groups = width // group
+    heads = group // HD
+    fetches = []
+    for t in range(3):
+        fetch = pltpu.make_async_copy(
+            q_all.at[pl.ds(t * width + here.j * group, group)], weights.at[t], sems.at[t]
+        )
+        fetch.start()
+        fetches.append(fetch)
+    vectors, hidden = spread_units(small[...], width, hid_out.shape[1])
+    vec_out[...] = vectors
+    hid_out[...] = hidden
+    gain, shift = vectors[0:1], vectors[1:2]
+    query_add = group_slice(vectors[2:3], here.j, groups)
+    value_add = group_slice(vectors[3:4], here.j, groups)
+    for fetch in fetches:
+        fetch.wait()
+
+    def project(p, carry):
+        source = block_at(spans, micro, p, blocks)
+        unit, scale = row_norm(x_all[source].astype(F32))
+        h = (unit * gain + shift).astype(BF)
+        at = pl.ds(pl.multiple_of(p * rows, 16), rows)
+        u_out[at, :] = unit.astype(BF)
+        h_out[at, :] = h
+        q_out[at, :] = (nt(h, weights[0]) + query_add).astype(BF)
+        k_out[at, :] = nt(h, weights[1]).astype(BF)
+        v_out[at, :] = (nt(h, weights[2]) + value_add).astype(BF)
+        return carry
+
+    lax.fori_loop(0, blocks, project, 0)
+
+    def attend(i, carry):
+        start = pl.multiple_of(i * QROWS, QROWS)
+        stacked = stack_heads(q_out[pl.ds(start, QROWS), :] * BF(score_scale), heads)
+
+        def step(kc, state):
+            top, total, acc = state
+            at = pl.ds(pl.multiple_of(kc * KCOLS, KCOLS), KCOLS)
+            bias = visible_bias(lens, micro, start, QROWS, kc * KCOLS, KCOLS)
+            scores = nt(stacked, k_out[at, :])
+            scores = (scores.reshape(heads, QROWS, KCOLS) + bias[None]).reshape(
+                heads * QROWS, KCOLS
+            )
+            new_top = jnp.maximum(top, jnp.max(scores, axis=1, keepdims=True))
+            probs = jnp.exp(scores - new_top)
+            factor = jnp.exp(top - new_top)
+            total = total * factor + jnp.sum(probs, axis=1, keepdims=True)
+            acc = acc * factor + nn(probs.astype(BF), v_out[at, :])
+            return new_top, total, acc
+
+        tall = heads * QROWS
+        top, total, acc = lax.fori_loop(
+            0,
+            (i * QROWS) // KCOLS + 1,
+            step,
+            (
+                jnp.full((tall, 1), masked_score, F32),
+                jnp.zeros((tall, 1), F32),
+                jnp.zeros((tall, group), F32),
+            ),
+        )
+        o_out[pl.ds(start, QROWS), :] = unstack_heads(acc / total, heads)
+        lse_out[i] = top + jnp.log(total)
+        return carry
+
+    lax.fori_loop(0, blocks * rows // QROWS, attend, 0)
+    for s in range(blocks):
+        at = pl.ds(pl.multiple_of(spans[0, micro, s] * rows, 16), rows)
+        ao[s] = o_out[at, :].astype(BF)
+
+
+def attend_forward(depth, lens, spans, x_all, q_all, f_all, hidden_total):
+    blocks, rows, width = x_all.shape
+    total = depth * 8
+    group = width // 4
+    pack_rows = blocks * rows
+    small_at = f_all.shape[1] // SMALL - 1
+    whole = lambda *dims: pl.BlockSpec(dims, lambda i: (0,) * len(dims))
+    heads = group // HD
+    outs = (
+        shape((blocks, rows, group), BF),
+        shape((pack_rows, group), BF),
+        shape((pack_rows, group), BF),
+        shape((pack_rows, group), BF),
+        shape((pack_rows, width), BF),
+        shape((pack_rows, width), BF),
+        shape((pack_rows, group), F32),
+        shape((pack_rows // QROWS, heads * QROWS, 1), F32),
+        shape((SMALL, width), F32),
+        shape((1, hidden_total), F32),
+    )
+    return pl.pallas_call(
+        functools.partial(forward_kernel, depth),
+        name="attend_forward",
+        grid=(1,),
+        out_shape=outs,
+        in_specs=[
+            smem(),
+            smem(),
+            whole(blocks, rows, width),
+            pl.BlockSpec((total, SMALL, width), lambda i: (0, small_at, 0)),
+            anywhere(),
+        ],
+        out_specs=tuple(whole(*o.shape) for o in outs),
+        scratch_shapes=[pltpu.VMEM((3, group, width), BF), pltpu.SemaphoreType.DMA((3,))],
+        compiler_params=params(),
+    )(lens, spans, x_all, f_all, q_all.reshape(-1, width))
+
+
+def middle_kernel(
+    x_ref,
+    dy_ref,
+    at_ref,
+    wo_ref,
+    up_ref,
+    down_ref,
+    vec_ref,
+    hid_ref,
+    y_out,
+    da_out,
+    dr_out,
+    grad_out,
+    go_out,
+    vec_out,
+    hid_out,
+    attn,
+    resid,
+    unit2,
+    h2,
+    scale2,
+    y_acc,
+    dh_acc,
+):
+    i = pl.program_id(0)
+    last = pl.num_programs(0) - 1
+    micros, rows, width = x_ref.shape
+    group = at_ref.shape[2]
+    devices, per = up_ref.shape[0], up_ref.shape[1]
+    chunk = devices * per
+    all_rows = micros * rows
+    g_down = dy_ref[...].reshape(all_rows, width)
+
+    @pl.when(i == 0)
+    def _():
+        for m in range(micros):
+            pieces = [at_ref[2 * j + m] for j in range(width // group)]
+            attn[m * rows : (m + 1) * rows, :] = jnp.concatenate(pieces, axis=1)
+        wo = wo_ref[...].reshape(width, width)
+        wide = x_ref[...].reshape(all_rows, width).astype(F32)
+        res = wide + nt(attn[...], wo) + vec_ref[4:5, :]
+        resid[...] = res
+        unit, scale = row_norm(res)
+        unit2[...] = unit
+        scale2[...] = scale
+        h2[...] = (unit * vec_ref[5:6, :] + vec_ref[6:7, :]).astype(BF)
+        y_acc[...] = jnp.zeros_like(y_acc)
+        dh_acc[...] = jnp.zeros_like(dh_acc)
+
+    up_w = up_ref[...].reshape(chunk, width)
+    down_w = down_ref[...].reshape(chunk, width)
+    up = nt(h2[...], up_w) + hid_ref[...]
+    square = up * up
+    tanh = jnp.tanh(GELU_A * (up + GELU_B * square * up))
+    half = 0.5 * (1.0 + tanh)
+    act = (up * half).astype(BF)
+    y_acc[...] += nn(act, down_w)
+    slope = half + 0.5 * up * (1.0 - tanh * tanh) * (GELU_A * (1.0 + 3.0 * GELU_B * square))
+    d_up32 = nt(g_down, down_w) * slope
+    d_up = d_up32.astype(BF)
+    hid_out[...] = jnp.sum(d_up.astype(F32), axis=0, keepdims=True)
+    dh_acc[...] += nn(d_up, up_w)
+    grad_out[:, 0:per, :] = tn(d_up, h2[...]).astype(BF).reshape(devices, per, width)
+    grad_out[:, per : 2 * per, :] = tn(act, g_down).astype(BF).reshape(devices, per, width)
+
+    @pl.when(i == last)
+    def _():
+        dy = g_down.astype(F32)
+        y = resid[...] + (y_acc[...] + vec_ref[7:8, :])
+        y_out[...] = y.astype(BF).reshape(micros, rows, width)
+        d_h2 = dh_acc[...]
+        unit = unit2[...]
+        d_res = dy + norm_back(d_h2 * vec_ref[5:6, :], unit, scale2[...])
+        dr_out[...] = d_res.reshape(micros, rows, width)
+        g_mix = d_res.astype(BF)
+        wo = wo_ref[...].reshape(width, width)
+        d_attn = nn(g_mix, wo).astype(BF)
+        for m in range(micros):
+            for j in range(width // group):
+                da_out[2 * j + m] = d_attn[m * rows : (m + 1) * rows, j * group : (j + 1) * group]
+        go_out[...] = tn(g_mix, attn[...]).astype(BF).reshape(go_out.shape)
+        zero = jnp.zeros((1, width), F32)
+        vec_out[...] = jnp.concatenate(
+            [
+                zero,
+                zero,
+                zero,
+                zero,
+                jnp.sum(g_mix.astype(F32), axis=0, keepdims=True),
+                jnp.sum(d_h2 * unit, axis=0, keepdims=True),
+                jnp.sum(d_h2, axis=0, keepdims=True),
+                jnp.sum(dy, axis=0, keepdims=True),
+            ],
+            axis=0,
+        )
+
+
+GELU_A = math.sqrt(2.0 / math.pi)
+GELU_B = 0.044715
+MIDDLE_DEVICES = 4
+
+
+def middle(x_own, dy_own, at_recv, f_all, vectors, hidden):
+    micros, rows, width = x_own.shape
+    total, f_rows, _ = f_all.shape
+    hidden_total = hidden.shape[1]
+    per = hidden_total // total
+    unit = width // total
+    chunk = MIDDLE_DEVICES * per
+    whole = lambda *dims: pl.BlockSpec(dims, lambda i: (0,) * len(dims))
+    all_rows = micros * rows
+    outs = (
+        shape((micros, rows, width), BF),
+        shape(at_recv.shape, BF),
+        shape((micros, rows, width), F32),
+        shape((total, 2 * per, width), BF),
+        shape((total, unit, width), BF),
+        shape((SMALL, width), F32),
+        shape((1, hidden_total), F32),
+    )
+    return pl.pallas_call(
+        middle_kernel,
+        name="middle",
+        grid=(total // MIDDLE_DEVICES,),
+        out_shape=outs,
+        in_specs=[
+            whole(micros, rows, width),
+            whole(micros, rows, width),
+            whole(*at_recv.shape),
+            pl.BlockSpec((total, unit, width), lambda i: (0, 2 * per // unit, 0)),
+            pl.BlockSpec((MIDDLE_DEVICES, per, width), lambda i: (i, 0, 0)),
+            pl.BlockSpec((MIDDLE_DEVICES, per, width), lambda i: (i, 1, 0)),
+            whole(SMALL, width),
+            pl.BlockSpec((1, chunk), lambda i: (0, i)),
+        ],
+        out_specs=(
+            whole(micros, rows, width),
+            whole(*at_recv.shape),
+            whole(micros, rows, width),
+            pl.BlockSpec((MIDDLE_DEVICES, 2 * per, width), lambda i: (i, 0, 0)),
+            whole(total, unit, width),
+            whole(SMALL, width),
+            pl.BlockSpec((1, chunk), lambda i: (0, i)),
+        ),
+        scratch_shapes=[
+            pltpu.VMEM((all_rows, width), BF),
+            pltpu.VMEM((all_rows, width), F32),
+            pltpu.VMEM((all_rows, width), F32),
+            pltpu.VMEM((all_rows, width), BF),
+            pltpu.VMEM((all_rows, 1), F32),
+            pltpu.VMEM((all_rows, width), F32),
+            pltpu.VMEM((all_rows, width), F32),
+        ],
+        compiler_params=params(),
+    )(x_own, dy_own, at_recv, f_all, f_all, f_all, vectors, hidden)
+
+
+def backward_kernel(
+    depth,
+    lens,
+    spans,
+    da_ref,
+    q_ref,
+    k_ref,
+    v_ref,
+    h_ref,
+    u_ref,
+    o_ref,
+    lse_ref,
+    vec_ref,
+    hid_ref,
+    q_all,
+    gq_out,
+    dh_out,
+    small_out,
+    weights,
+    da,
+    dq_acc,
+    dk_acc,
+    dv_acc,
+    dq,
+    dk,
+    dv,
+    sums,
+    sems,
+):
+    here = Place(depth)
+    micro = here.core
+    blocks, rows, group = da_ref.shape
+    width = h_ref.shape[1]
+    groups = width // group
+    heads = group // HD
+    pack_rows = blocks * rows
+    fetches = []
+    for t in range(3):
+        fetch = pltpu.make_async_copy(
+            q_all.at[pl.ds(t * width + here.j * group, group)], weights.at[t], sems.at[t]
+        )
+        fetch.start()
+        fetches.append(fetch)
+    for p in range(blocks):
+        da[p * rows : (p + 1) * rows, :] = da_ref[block_at(spans, micro, p, blocks)]
+    dk_acc[...] = jnp.zeros_like(dk_acc)
+    dv_acc[...] = jnp.zeros_like(dv_acc)
+
+    def query_block(i, carry):
+        start = pl.multiple_of(i * QROWS, QROWS)
+        at_q = pl.ds(start, QROWS)
+        stacked = stack_heads(q_ref[at_q, :] * BF(score_scale), heads)
+        d_rows = da[at_q, :]
+        d_stacked = stack_heads(d_rows, heads)
+        product = d_rows.astype(F32) * o_ref[at_q, :]
+        delta = jnp.sum(stack_heads(product, heads), axis=1, keepdims=True)
+        lse = lse_ref[i]
+
+        def step(kc, acc):
+            at = pl.ds(pl.multiple_of(kc * KCOLS, KCOLS), KCOLS)
+            bias = visible_bias(lens, micro, start, QROWS, kc * KCOLS, KCOLS)
+            keys = k_ref[at, :]
+            scores = nt(stacked, keys)
+            scores = (scores.reshape(heads, QROWS, KCOLS) + bias[None]).reshape(
+                heads * QROWS, KCOLS
+            )
+            probs = jnp.exp(scores - lse)
+            d_probs = nt(d_stacked, v_ref[at, :])
+            d_scores = (probs * (d_probs - delta)).astype(BF)
+            dk_acc[at, :] += tn(d_scores, stacked)
+            dv_acc[at, :] += tn(probs.astype(BF), d_stacked)
+            return acc + nn(d_scores, keys)
+
+        acc = lax.fori_loop(
+            0, (i * QROWS) // KCOLS + 1, step, jnp.zeros((heads * QROWS, group), F32)
+        )
+        dq_acc[at_q, :] = unstack_heads(acc, heads) * score_scale
+        return carry
+
+    lax.fori_loop(0, pack_rows // QROWS, query_block, 0)
+    dq[...] = dq_acc[...].astype(BF)
+    dk[...] = dk_acc[...].astype(BF)
+    dv[...] = dv_acc[...].astype(BF)
+    for t, part in enumerate((dq, dk, dv)):
+        gq_out[t] = tn(part[...], h_ref[...]).astype(BF).reshape(gq_out.shape[1:])
+    query_bias = jnp.sum(dq[...].astype(F32), axis=0, keepdims=True)
+    value_bias = jnp.sum(dv[...].astype(F32), axis=0, keepdims=True)
+    for fetch in fetches:
+        fetch.wait()
+    sums[...] = jnp.zeros_like(sums)
+
+    def unsort(s, carry):
+        at = pl.ds(pl.multiple_of(spans[0, micro, s] * rows, 16), rows)
+        part = (
+            nn(dq[at, :], weights[0]) + nn(dk[at, :], weights[1]) + nn(dv[at, :], weights[2])
+        )
+        dh_out[s] = part.astype(BF)
+        sums[0:1, :] += jnp.sum(part * u_ref[at, :].astype(F32), axis=0, keepdims=True)
+        sums[1:2, :] += jnp.sum(part, axis=0, keepdims=True)
+        return carry
+
+    lax.fori_loop(0, blocks, unsort, 0)
+    vectors = jnp.concatenate(
+        [
+            sums[0:2, :],
+            group_spread(query_bias, here.j, groups),
+            group_spread(value_bias, here.j, groups),
+            vec_ref[4:8, :],
+        ],
+        axis=0,
+    )
+    left, right = gather_units(vectors, hid_ref[...], depth * 8)
+    small_out[...] = jnp.zeros_like(small_out)
+    small_out[:, :, 0:128] = left
+    small_out[:, :, 128:256] = right
+
+
+def attend_backward(depth, lens, spans, da_recv, saved, vec_grads, hid_grads, q_all):
+    q, k, v, h, u, o, lse = saved
+    blocks, rows, group = da_recv.shape
+    pack_rows, width = h.shape
+    total = depth * 8
+    unit = width // total
+    wide = lambda dtype: pltpu.VMEM((pack_rows, group), dtype)
+    return pl.pallas_call(
+        functools.partial(backward_kernel, depth),
+        name="attend_backward",
+        out_shape=(
+            shape((3, group // unit, unit, width), BF),
+            shape((blocks, rows, width), BF),
+            shape((total, SMALL, width), BF),
+        ),
+        in_specs=[smem(), smem()] + [vmem()] * 10 + [anywhere()],
+        out_specs=(vmem(),) * 3,
+        scratch_shapes=[
+            pltpu.VMEM((3, group, width), BF),
+            wide(BF),
+            wide(F32),
+            wide(F32),
+            wide(F32),
+            wide(BF),
+            wide(BF),
+            wide(BF),
+            pltpu.VMEM((SMALL, width), F32),
+            pltpu.SemaphoreType.DMA((3,)),
+        ],
+        compiler_params=params(),
+    )(lens, spans, da_recv, q, k, v, h, u, o, lse, vec_grads, hid_grads, q_all.reshape(-1, width))
+
+
+def reduce_kernel(
+    depth,
+    grad_ref,
+    out_ref,
+    small_ref,
+    gq_ref,
+    dh_ref,
+    f_sum,
+    q_sum,
+    dh_sum,
+    held,
+    from_mate,
+    from_one,
+    from_two,
+    from_below,
+    from_above,
+    q_held,
+    q_mate,
+    q_line,
+    dh_recv,
+    load_sem,
+    csend,
+    crecv,
+    send1,
+    recv1,
+    send2,
+    recv2,
+    zsend,
+    zrecv_up,
+    zrecv_down,
+    qc_sem,
+    q_send,
+    q_recv,
+    dh_send,
+    dh_recv_sem,
+):
+    here = Place(depth)
+    z, r = here.z, here.r
+    a, b, core, j = here.a, here.b, here.core, here.j
+    half = held.shape[4]
+    width = held.shape[5]
+    per = grad_ref.shape[4] // 2
+    unit = out_ref.shape[4]
+    greet_all(here)
+
+    spans = (
+        ((grad_ref, 0, per, 0), (out_ref, 0, half - per, per)),
+        (
+            (grad_ref, per, per, 0),
+            (out_ref, half - per, unit - (half - per), per),
+            (small_ref, 0, SMALL, per + unit - (half - per)),
+        ),
+    )
+
+    def order(k):
+        out = jnp.int32(0)
+        for zz in range(depth):
+            line = sorted(range(depth), key=lambda t: (-abs(t - zz), t))
+            out = jnp.where(z == zz, line[k], out)
+        return out
+
+    def pieces(p, t, which, target):
+        for n, (ref, start, rows, at) in enumerate(spans[p]):
+            yield n, ref.at[t, :, :, which, pl.ds(start, rows)], target.at[
+                p, t, :, :, pl.ds(at, rows)
+            ]
+
+    for k in range(depth):
+        t = order(k)
+        for p in range(2):
+            for n, source, target in pieces(p, t, 1 - core, from_mate):
+                remote(source, target, csend.at[p, t, n], crecv.at[p, t, n], z, here.mate).start()
+            for n, source, target in pieces(p, t, core, held):
+                pltpu.make_async_copy(source, target, load_sem.at[p, t, n]).start()
+
+    for k in range(1, 8):
+        to = (r + k) % 8
+        remote(
+            dh_ref.at[to], dh_recv.at[r], dh_send.at[to], dh_recv_sem.at[r], z, to
+        ).start()
+    own_dh = pltpu.make_async_copy(dh_ref.at[r], dh_recv.at[r], dh_send.at[r])
+    own_dh.start()
+
+    to_mate = remote(
+        gq_ref.at[:, :, 1 - core], q_mate, qc_sem.at[0], qc_sem.at[1], z, here.mate
+    )
+    to_mate.start()
+    keep = pltpu.make_async_copy(gq_ref.at[:, :, core], q_held, qc_sem.at[2])
+    keep.start()
+    keep.wait()
+    to_mate.wait_recv()
+    kinds, pairs = q_held.shape[0], q_held.shape[1]
+    for kind in range(kinds):
+        for m in range(pairs):
+            q_held[kind, m] = (
+                q_held[kind, m].astype(F32) + q_mate[kind, m].astype(F32)
+            ).astype(BF)
+
+    units_each = 3
+    per_kind = depth * 8 * units_each // kinds
+
+    def q_route(kind, m):
+        block = kind * per_kind + j * (pairs * 2) + m * 2 + core
+        owner = block // units_each
+        return owner // 8, owner % 8, block % units_each
+
+    def q_moves(act_remote, act_local):
+        for kind in range(kinds):
+            for m in range(pairs):
+                oz, orr, at = q_route(kind, m)
+                mine = (oz == z) & (orr == r)
+
+                @pl.when(jnp.logical_not(mine))
+                def _():
+                    act_remote(
+                        remote(
+                            q_held.at[kind, m],
+                            q_line.at[at, z],
+                            q_send.at[kind, m],
+                            q_recv.at[at, z],
+                            oz,
+                            orr,
+                        )
+                    )
+
+                @pl.when(mine)
+                def _():
+                    act_local(
+                        pltpu.make_async_copy(
+                            q_held.at[kind, m], q_line.at[at, z], q_send.at[kind, m]
+                        )
+                    )
+
+    q_moves(lambda c: c.start(), lambda c: c.start())
+
+    def add(target, source):
+        target[...] = (target[...].astype(F32) + source[...].astype(F32)).astype(BF)
+
+    def add_blocks(pairs_of_refs):
+        for target, source in pairs_of_refs:
+            add(target, source)
+
+    def stage_mate(t):
+        for p in range(2):
+            for n, source, target in pieces(p, t, core, held):
+                pltpu.make_async_copy(source, target, load_sem.at[p, t, n]).wait()
+            for n, source, target in pieces(p, t, 1 - core, from_mate):
+                remote(
+                    source, target, csend.at[p, t, n], crecv.at[p, t, n], z, here.mate
+                ).wait_recv()
+            for aa in range(2):
+                for bb in range(2):
+                    add(held.at[p, t, aa, bb], from_mate.at[p, t, aa, bb])
+        first(0, t).start()
+        first(1, t).start()
+
+    def first(p, t):
+        if p == 0:
+            return remote(
+                held.at[0, t, 1 - a], from_one.at[0, t], send1.at[0, t], recv1.at[0, t], z, here.by_a
+            )
+        return remote(
+            held.at[1, t, :, 1 - b], from_one.at[1, t], send1.at[1, t], recv1.at[1, t], z, here.by_b
+        )
+
+    def second(p, t):
+        if p == 0:
+            return remote(
+                held.at[0, t, a, 1 - b],
+                from_two.at[0, t],
+                send2.at[0, t],
+                recv2.at[0, t],
+                z,
+                here.by_b,
+            )
+        return remote(
+            held.at[1, t, 1 - a, b], from_two.at[1, t], send2.at[1, t], recv2.at[1, t], z, here.by_a
+        )
+
+    def stage_one(t):
+        for p in range(2):
+            first(p, t).wait_recv()
+            for n in range(2):
+                mine = held.at[0, t, a, n] if p == 0 else held.at[1, t, n, b]
+                add(mine, from_one.at[p, t, n])
+            second(p, t).start()
+
+    def upward(p, t):
+        return remote(
+            held.at[p, t, a, b],
+            from_below.at[p, t],
+            zsend.at[p, t],
+            zrecv_up.at[p, t],
+            z + 1,
+            r,
+        )
+
+    def downward(p, t):
+        return remote(
+            held.at[p, t, a, b],
+            from_above.at[p, t],
+            zsend.at[p, t],
+            zrecv_down.at[p, t],
+            z - 1,
+            r,
+        )
+
+    def stage_two(t):
+        for p in range(2):
+            mine = held.at[p, t, a, b]
+            second(p, t).wait_recv()
+            add(mine, from_two.at[p, t])
+
+            @pl.when((t >= z) & (z > 0))
+            def _():
+                upward(p, t).wait_recv()
+                add(mine, from_below.at[p, t])
+
+            @pl.when((t <= z) & (z < depth - 1))
+            def _():
+                downward(p, t).wait_recv()
+                add(mine, from_above.at[p, t])
+
+            @pl.when(t > z)
+            def _():
+                upward(p, t).start()
+
+            @pl.when(t < z)
+            def _():
+                downward(p, t).start()
+
+    for step in range(depth + 2):
+        if step < depth:
+            stage_mate(order(step))
+        if 0 <= step - 1 < depth:
+            stage_one(order(step - 1))
+        if 0 <= step - 2 < depth:
+            stage_two(order(step - 2))
+    for p in range(2):
+        f_sum[p] = held[p, z, a, b].astype(F32)
+
+    own_dh.wait()
+    for k in range(1, 8):
+        frm = (r + k) % 8
+        remote(
+            dh_ref.at[frm], dh_recv.at[frm], dh_send.at[frm], dh_recv_sem.at[frm], z, frm
+        ).wait()
+    for m in range(2):
+        part = dh_recv[m].astype(F32)
+        for chip in range(1, 4):
+            part = part + dh_recv[2 * chip + m].astype(F32)
+        dh_sum[m] = part
+
+    me = here.slot(z, r)
+    for at in range(units_each):
+        block = me * units_each + at
+        inside = block % per_kind
+        from_r = (inside // (pairs * 2)) * 2 + inside % 2
+        for zz in range(depth):
+            @pl.when(jnp.logical_not((from_r == r) & (zz == z)))
+            def _():
+                remote(
+                    q_held.at[0, 0], q_line.at[at, zz], q_send.at[0, 0], q_recv.at[at, zz], zz, from_r
+                ).wait_recv()
+    q_moves(lambda c: c.wait_send(), lambda c: c.wait())
+    for at in range(units_each):
+        part = q_line[at, 0].astype(F32)
+        for zz in range(1, depth):
+            part = part + q_line[at, zz].astype(F32)
+        q_sum[at] = part
+
+    to_mate.wait_send()
+    for t in range(depth):
+        for p in range(2):
+            for n, source, target in pieces(p, t, 1 - core, from_mate):
+                remote(
+                    source, target, csend.at[p, t, n], crecv.at[p, t, n], z, here.mate
+                ).wait_send()
+            first(p, t).wait_send()
+            second(p, t).wait_send()
+
+            @pl.when(z != t)
+            def _():
+                upward(p, t).wait_send()
+
+
+def reduce(depth, grads, out_grads, small, gq, dh):
+    total, two_per, width = grads.shape
+    per = two_per // 2
+    unit = out_grads.shape[1]
+    half = (two_per + unit + SMALL) // 2
+    kinds, units, _, _ = gq.shape
+    rows = dh.shape[1]
+    dma = pltpu.SemaphoreType.DMA
+    line = lambda ref: ref.reshape((depth, 2, 2, 2) + ref.shape[1:])
+    return pl.pallas_call(
+        functools.partial(reduce_kernel, depth),
+        name="reduce",
+        out_shape=(
+            shape((2, half, width), F32),
+            shape((3, unit, width), F32),
+            shape((2, rows, width), F32),
+        ),
+        in_specs=[anywhere()] * 5,
+        out_specs=(vmem(),) * 3,
+        scratch_shapes=[
+            pltpu.VMEM((2, depth, 2, 2, half, width), BF),
+            pltpu.VMEM((2, depth, 2, 2, half, width), BF),
+            pltpu.VMEM((2, depth, 2, half, width), BF),
+            pltpu.VMEM((2, depth, half, width), BF),
+            pltpu.VMEM((2, depth, half, width), BF),
+            pltpu.VMEM((2, depth, half, width), BF),
+            pltpu.VMEM((kinds, units // 2, unit, width), BF),
+            pltpu.VMEM((kinds, units // 2, unit, width), BF),
+            pltpu.VMEM((3, depth, unit, width), BF),
+            pltpu.VMEM((8, rows, width), BF),
+            dma((2, depth, 3)),
+            dma((2, depth, 3)),
+            dma((2, depth, 3)),
+            dma((2, depth)),
+            dma((2, depth)),
+            dma((2, depth)),
+            dma((2, depth)),
+            dma((2, depth)),
+            dma((2, depth)),
+            dma((2, depth)),
+            dma((3,)),
+            dma((kinds, units // 2)),
+            dma((3, depth)),
+            dma((8,)),
+            dma((8,)),
+        ],
+        compiler_params=params(4),
+    )(
+        line(grads),
+        line(out_grads),
+        line(small),
+        gq.reshape(kinds, units // 2, 2, unit, width),
+        dh,
+    )
+
+
+def final_kernel(
+    tie,
+    x_ref,
+    dh_ref,
+    dr_ref,
+    vec_ref,
+    f_ref,
+    q_ref,
+    dx_out,
+    g1,
+    s1,
+    wq,
+    bq,
+    bv,
+    wo,
+    bo,
+    g2,
+    s2,
+    wu,
+    bu,
+    wd,
+    bd,
+):
+    micros = x_ref.shape[0]
+    for m in range(micros):
+        unit, scale = row_norm(x_ref[m].astype(F32))
+        back = norm_back(dh_ref[m] * vec_ref[0:1, :], unit, scale)
+        dx_out[m] = (dr_ref[m] + back).astype(BF)
+    layers = wq.shape[0]
+    per = wu.shape[2]
+    unit = wo.shape[2]
+    half = f_ref.shape[1]
+    width = wq.shape[1]
+
+    def put(ref, index, value):
+        for layer in range(layers):
+            ref[layer] = jnp.where(tie[index] == layer, value, 0.0)
+
+    put(wu, 9, f_ref[0, 0:per, :].T)
+    put(wd, 11, f_ref[1, 0:per, :])
+    split = half - per
+    out_rows = jnp.concatenate(
+        [f_ref[0, per:half, :], f_ref[1, per : per + unit - split, :]], axis=0
+    )
+    put(wo, 5, out_rows.T)
+    put(wq, 2, q_ref[...].reshape(3 * unit, width).T)
+    small = f_ref[1, per + unit - split :, :]
+    names = ((g1, 0), (s1, 1), (bq, 3), (bv, 4), (bo, 6), (g2, 7), (s2, 8), (bd, 12))
+    for n, (ref, index) in enumerate(names):
+        for layer in range(layers):
+            ref[layer : layer + 1, :] = jnp.where(
+                tie[index] == layer, small[n : n + 1, 0:unit], 0.0
+            )
+    for layer in range(layers):
+        bu[layer : layer + 1, :] = jnp.where(tie[10] == layer, small[0:1, 128 : 128 + per], 0.0)
+
+
+def finish(tie_map, x_own, dh_sum, d_resid, vectors, f_sum, q_sum, banks):
+    outs = (shape(x_own.shape, BF),) + tuple(shape(bank.shape, F32) for bank in banks)
+    return pl.pallas_call(
+        final_kernel,
+        name="finish",
+        out_shape=outs,
+        in_specs=[smem()] + [vmem()] * 6,
+        out_specs=(vmem(),) * len(outs),
+        compiler_params=params(),
+    )(tie_map, x_own, dh_sum, d_resid, vectors, f_sum, q_sum)
+
+
+def grouped_plan(depth, *args):
+    block_input, cotangent, tie_map, seq_lengths, span_place = args[:5]
+    banks = args[5:]
+    x_own, dy_own = block_input[0], cotangent[0]
+    f_own, q_own = pack(tie_map, banks)
+    q_all, f_all, x_all = gather(depth, q_own, f_own, x_own)
+    hidden_total = banks[10].shape[1] * depth * 8
+    ao, q, k, v, h, u, o, lse, vectors, hidden = attend_forward(
+        depth, seq_lengths, span_place, x_all, q_all, f_all, hidden_total
+    )
+    at_recv = exchange(depth, ao, 2)
+    y, da, d_resid, grads, out_grads, vec_grads, hid_grads = middle(
+        x_own, dy_own, at_recv, f_all, vectors, hidden
+    )
+    da_recv = exchange(depth, da, 3)
+    gq, dh, small = attend_backward(
+        depth, seq_lengths, span_place, da_recv, (q, k, v, h, u, o, lse), vec_grads, hid_grads, q_all
+    )
+    f_sum, q_sum, dh_sum = reduce(depth, grads, out_grads, small, gq, dh)
+    final = finish(tie_map, x_own, dh_sum, d_resid, vectors, f_sum, q_sum, banks)
+    return (y[None], final[0][None]) + tuple(final[1:])
+def fits_grouped(mesh, block_input, span_place, qkv_weight):
+    width = qkv_weight.shape[1]
+    rows = block_input.shape[2] // mesh.shape["ctx"]
+    total = mesh.shape["ctx"] * mesh.shape["dp"]
+    return (
+        mesh.shape["ctx"] == 8
+        and block_input.shape[1] == 2
+        and HEADS % 4 == 0
+        and HEADS * HD == width
+        and rows % 16 == 0
+        and block_input.shape[2] % KCOLS == 0
+        and width % total == 0
+        and (width // total) % 8 == 0
+        and (width // 4) % (2 * (width // total)) == 0
+    )
+
+
 def solution(mesh):
-    placed = (
-        P("dp", None, "ctx", None),
-        P("dp", None, "ctx", None),
-        P(),
-        P("dp", None, None),
-        P("dp", None, None),
-        P(None, ("dp", "ctx")),
-        P(None, ("dp", "ctx")),
-        P(None, None, ("dp", "ctx")),
-        P(None, ("dp", "ctx")),
-        P(None, ("dp", "ctx")),
-        P(None, None, ("dp", "ctx")),
-        P(None, ("dp", "ctx")),
-        P(None, ("dp", "ctx")),
-        P(None, ("dp", "ctx")),
-        P(None, None, ("dp", "ctx")),
-        P(None, ("dp", "ctx")),
+    replicated_rows = P("dp", None, "ctx", None)
+    vector = P(None, ("dp", "ctx"))
+    columns = P(None, None, ("dp", "ctx"))
+    bank_specs = (
+        vector,
+        vector,
+        columns,
+        vector,
+        vector,
+        columns,
+        vector,
+        vector,
+        vector,
+        columns,
+        vector,
         P(None, ("dp", "ctx"), None),
-        P(None, ("dp", "ctx")),
-    )
-    return jax.shard_map(
-        on_device,
-        mesh=mesh,
-        in_specs=placed,
-        out_specs=(
-            P("dp", None, "ctx", None),
-            P("dp", None, "ctx", None),
-            P(None, ("dp", "ctx")),
-            P(None, ("dp", "ctx")),
-            P(None, None, ("dp", "ctx")),
-            P(None, ("dp", "ctx")),
-            P(None, ("dp", "ctx")),
-            P(None, None, ("dp", "ctx")),
-            P(None, ("dp", "ctx")),
-            P(None, ("dp", "ctx")),
-            P(None, ("dp", "ctx")),
-            P(None, None, ("dp", "ctx")),
-            P(None, ("dp", "ctx")),
-            P(None, ("dp", "ctx"), None),
-            P(None, ("dp", "ctx")),
-        ),
-        check_vma=False,
-    )
+        vector,
+    )
+
+    def step(*args):
+        if fits_grouped(mesh, args[0], args[4], args[7]):
+            plan = functools.partial(grouped_plan, mesh.shape["dp"])
+        else:
+            plan = general_plan
+        return jax.shard_map(
+            plan,
+            mesh=mesh,
+            in_specs=(
+                replicated_rows,
+                replicated_rows,
+                P(),
+                P("dp", None, None),
+                P("dp", None, None),
+            )
+            + bank_specs,
+            out_specs=(replicated_rows, replicated_rows) + bank_specs,
+            check_vma=False,
+        )(*args)
+
+    return step

time: 1190 us -> 294 us (0.25); the launches traced: 1170 us -> 289 us
  waiting for transfers between devices: 427 us -> 0 us
  Pallas kernels: 0 us -> 277 us
  matrix products: 249 us -> 0 us
  local copies, waits for them, and re-layouts: 165 us -> 10.9 us
  other arithmetic: 143 us -> 0 us
  blocking collectives: 116 us -> 0 us
  between operations: 41.4 us -> 0.71 us
  loops' own time: 27.3 us -> 0 us
    reduce_scatter x4 -> x0, waiting for transfers between devices: 322 us -> none  [the longest x1 140 us: on_device(): lax.psum_scatter(totals[11], ('dp', 'ctx'), scatter_dimension=0, tiled=True)]
    pallas_call x0 -> x9, Pallas kernels: none -> 277 us  [the longest x1 86.6 us: gather(): pl.pallas_call(functools.partial(gather_kernel, depth, pieces), name='gat...]
    dot_general x150 -> x0, matrix products: 249 us -> none  [the longest x18 44.5 us: mutual(): jnp.einsum('hqk,qhd->khd', probs_other, gradout_heads, preferred_element_...]
    all_gather x12 -> x0, waiting for transfers between devices: 103 us -> none  [the longest x1 49.3 us: on_device(): lax.all_gather(shards[11], ('dp', 'ctx'), axis=0, tiled=True)]
    dynamic_slice x130 -> x0, local copies, waits for them, and re-layouts: 101 us -> none  [the longest x126 97.9 us: over_blocks(): lax.scan(inner_step, state, (jnp.arange(piece_rows // block_rows, dtype=j...]
    unnamed x2 -> x0, blocking collectives: 79.9 us -> none
    reduce_sum x106 -> x0, other arithmetic: 76.8 us -> none  [the longest x38 28.8 us: segment_ids(): jnp.sum((positions[:, None] >= seq_ends[None, :]).astype(jnp.int32), axis=1)]
    and x54 -> x0, other arithmetic: 42.7 us -> none  [the longest x36 28.4 us: score_probs(): (query_seg[:, None] == key_seg[None, :]) & (key_pos[None, :] <= query_pos...]
  transfers between devices with their start and end apart: 16 -> 0, of which waited for: 7 -> 0; matrix products, arithmetic and copies ran while one was open for 46% -> 0% of each run, Pallas kernels for 0% -> 0%
where the time goes in v1:
time: 294 us; the launch traced here: 289 us
  Pallas kernels  277 us (94%)
  local copies, waits for them, and re-layouts  10.9 us (4%)
    pallas_call x1, Pallas kernels, gather(): pl.pallas_call(functools.partial(gather_kernel, depth, pieces), name='gat...  86.6 us
    pallas_call x1, Pallas kernels, reduce(): pl.pallas_call(functools.partial(reduce_kernel, depth), name='reduce', ou...  82.7 us
    pallas_call x1, Pallas kernels, attend_backward(): pl.pallas_call(functools.partial(backward_kernel, depth), name='attend_ba...  28.1 us
    pallas_call x1, Pallas kernels, attend_forward(): pl.pallas_call(functools.partial(forward_kernel, depth), name='attend_for...  26.2 us
    pallas_call x2, Pallas kernels, exchange(): pl.pallas_call(functools.partial(exchange_kernel, depth), name='exchange'...  23.5 us
    pallas_call x1, Pallas kernels, middle(): pl.pallas_call(middle_kernel, name='middle', grid=(total // MIDDLE_DEVICE...  23.3 us
    unnamed x8, local copies, waits for them, and re-layouts  10.9 us

profile of v1, /device:TPU:23, one launch (start us, length us, event | category | flops | bytes accessed | tf_op | source)
XLA Modules:
  0.0 288.9 jit_solution(12211924809483889748)
XLA Ops:
  0.6 1.9 copy.33.wq
  2.5 1.8 copy.34.wo
  4.3 1.9 copy.35.wu
  6.2 2.3 pack.1
  8.5 86.6 %gather.1 = (bf16[32,72,768]{2,1,0:T(8,128)(2,1)}, bf16[32,224,768]{2,1,0:T(8,128)(2,1)}, bf16[8,144,768]{2,1,0:T(8,128)(2,1)}) custom-call(bf16[72,768]{1,0:T(8,128)(2,1)} %get-tuple-element.57.q_in, bf16[224,768]{1,0:T(8,128)(2,1)} %get-tuple-element.58.f_in, bf16[2,144,768]{2,1,0:T(8,128)(2,1)} %bitcast.12), custom_call_target="tpu_custom_call" | custom-call | tf_op jit(solution)/shard_map/gather/pallas_call | solution.py:778
  95.2 26.2 %attend_forward.1 = (bf16[8,144,192]{2,1,0:T(8,128)(2,1)}, bf16[1152,192]{1,0:T(8,128)(2,1)}, bf16[1152,192]{1,0:T(8,128)(2,1)}, bf16[1152,192]{1,0:T(8,128)(2,1...) custom-call(s32[1,2,4]{2,1,0:T(2,128)} %lens.3, ...), custom_call_target="tpu_custom_call" | custom-call | tf_op jit(solution)/shard_map/attend_forward/pallas_call | solution.py:1061
  121.3 11.8 %exchange.2.at_ref = bf16[8,144,192]{2,1,0:T(8,128)(2,1)} custom-call(bf16[8,144,192]{2,1,0:T(8,128)(2,1)} %get-tuple-element.62.block), custom_call_target="tpu_custom_call" | custom-call | tf_op jit(solution)/shard_map/exchange/pallas_call | solution.py:822
  133.1 23.3 %middle.1 = (bf16[2,144,768]{2,1,0:T(8,128)(2,1)}, bf16[8,144,192]{2,1,0:T(8,128)(2,1)}, f32[2,144,768]{2,1,0:T(8,128)}, bf16[32,192,768]{2,1,0:T(8,128)(2,1)}, ...) custom-call(bf16[2,144,768]{2,1,0:T(8,128)(2,1)} %bitcast.13, bf16[2,144,768]{2,1,0:T(8,128)(2,1)} %bitcast.17, ...), custom_call_target="tpu_custom_call" | custom-call | tf_op jit(solution)/shard_map/middle/pallas_call | solution.py:1199
  156.5 11.8 %exchange.3.da_ref = bf16[8,144,192]{2,1,0:T(8,128)(2,1)} custom-call(bf16[8,144,192]{2,1,0:T(8,128)(2,1)} %get-tuple-element.68.block), custom_call_target="tpu_custom_call" | custom-call | tf_op jit(solution)/shard_map/exchange/pallas_call | solution.py:822
  168.2 28.1 %attend_backward.1 = (bf16[3,8,24,768]{3,2,1,0:T(8,128)(2,1)}, bf16[8,144,768]{2,1,0:T(8,128)(2,1)}, bf16[32,8,768]{2,1,0:T(8,128)(2,1)}) custom-call(s32[1,2,4]{2,1,0:T(2,128)} %lens.3, s32[1,2,8]{2,1,0:T(2,128)} %spans.3, bf16[8,144,192]{2,1,0:T(8,128)(2,1)} %exchange.3.da_ref, bf16[1152,192]{1,0:T(8,128)(2,1)} %get-tuple-element.69.q_ref, ...), custom_call_target="tpu_custom_call" | custom-call | tf_op jit(solution)/shard_map/attend_backward/pallas_call | solution.py:1360
  196.4 82.7 %reduce.1 = (f32[2,112,768]{2,1,0:T(8,128)}, f32[3,24,768]{2,1,0:T(8,128)}, f32[2,144,768]{2,1,0:T(8,128)}) custom-call(bf16[4,2,2,2,192,768]{5,4,3,2,1,0:T(8,128)(2,1)} %bitcast.11, bf16[4,2,2,2,24,768]{5,4,3,2,1,0:T(8,128)(2,1)} %bitcast.15, bf16[4,2,2,2,8,768]{5,4,3,2,1,0:T(8,128)(2,1)} %bitcast.18, bf16[3,4,2,24,768]{4,3,2,1,0:T(8,128)(2,1)} %bitcast.16, ...), custom_call_target="tpu_custom_call" | custom-call | tf_op jit(solution)/shard_map/reduce/pallas_call | solution.py:1681
  279.1 4.4 %finish.1 = (bf16[2,144,768]{2,1,0:T(8,128)(2,1)}, f32[2,24]{1,0:T(2,128)}, f32[2,24]{1,0:T(2,128)}, f32[2,768,72]{2,1,0:T(8,128)}, f32[2,24]{1,0:T(2,128)}, /*i...) custom-call(s32[13]{0:T(128)} %tie.3, ...), custom_call_target="tpu_custom_call" | custom-call | tf_op jit(solution)/shard_map/finish/pallas_call | solution.py:1787
  283.5 0.0 copy-start
  283.5 2.1 copy.37
  285.6 2.1 copy.36
  287.8 0.0 copy-done
  287.8 1.1 copy.38
Async XLA Ops:
  283.5 4.3 %copy-start = (f32[2,768,96]{2,1,0:T(8,128)S(1)}, f32[2,768,96]{2,1,0:T(8,128)}, u32[]{:S(2)}) copy-start(f32[2,768,96]{2,1,0:T(8,128)} %get-tuple-element.110) | copy-start | bytes 1769476

commit v2 on v0

--- a/solution.py
+++ b/solution.py
@@ -1,8 +1,12 @@
+import functools
 import math
+import types
 
 import jax
 import jax.numpy as jnp
 from jax import lax
+from jax.experimental import pallas as pl
+from jax.experimental.pallas import tpu as pltpu
 from jax.sharding import PartitionSpec as P
 
 HEADS = 12
@@ -82,7 +86,7 @@
     return (probs.astype(jnp.bfloat16), dscores)
 
 
-def on_device(
+def general_plan(
     block_input,
     cotangent,
     tie_map,
@@ -442,47 +446,1233 @@
     return (block_output, input_grad) + bank_grads
 
 
+BF = jnp.bfloat16
+F32 = jnp.float32
+MESH = pl.DeviceIdType.MESH
+ANY = pl.ANY
+SMALL = 8
+VMEM_BYTES = 62 * 2**20
+
+
+def params(collective_id=None):
+    if collective_id is None:
+        return pltpu.CompilerParams(vmem_limit_bytes=VMEM_BYTES)
+    return pltpu.CompilerParams(
+        vmem_limit_bytes=VMEM_BYTES, collective_id=collective_id, has_side_effects=True
+    )
+
+
+def vmem():
+    return pl.BlockSpec(memory_space=pltpu.VMEM)
+
+
+def smem():
+    return pl.BlockSpec(memory_space=pltpu.SMEM)
+
+
+def anywhere():
+    return pl.BlockSpec(memory_space=ANY)
+
+
+def shape(dims, dtype):
+    return jax.ShapeDtypeStruct(dims, dtype)
+
+
+def nn(left, right):
+    return lax.dot_general(left, right, (((1,), (0,)), ((), ())), preferred_element_type=F32)
+
+
+def nt(left, right):
+    return lax.dot_general(left, right, (((1,), (1,)), ((), ())), preferred_element_type=F32)
+
+
+def tn(left, right):
+    return lax.dot_general(left, right, (((0,), (0,)), ((), ())), preferred_element_type=F32)
+
+
+def iota(dims, axis):
+    return lax.broadcasted_iota(jnp.int32, dims, axis)
+
+
+class Place:
+    def __init__(self, depth):
+        self.depth = depth
+        self.z = lax.axis_index("dp")
+        self.r = lax.axis_index("ctx")
+        self.core = self.r % 2
+        self.j = self.r // 2
+        self.a = self.r // 4
+        self.b = (self.r // 2) % 2
+        self.by_a = (1 - self.a) * 4 + self.b * 2 + self.core
+        self.by_b = self.a * 4 + (1 - self.b) * 2 + self.core
+        self.both = (1 - self.a) * 4 + (1 - self.b) * 2 + self.core
+        self.mate = self.j * 2 + 1 - self.core
+
+    def slot(self, z, r):
+        return z * 8 + r
+
+
+def greet_all(here):
+    bar = pltpu.get_barrier_semaphore()
+    total = here.depth * 8
+    me = here.z * 8 + here.r
+
+    def signal(k, carry):
+        other = (me + k) % total
+        pl.semaphore_signal(bar, inc=1, device_id=(other // 8, other % 8), device_id_type=MESH)
+        return carry
+
+    lax.fori_loop(1, total, signal, 0)
+    pl.semaphore_wait(bar, total - 1)
+
+
+def remote(source, target, send, recv, z, r):
+    return pltpu.make_async_remote_copy(
+        src_ref=source,
+        dst_ref=target,
+        send_sem=send,
+        recv_sem=recv,
+        device_id=(z, r),
+        device_id_type=MESH,
+    )
+
+
+def spread_units(small, width, hidden_total):
+    devices = small.shape[0]
+    unit = width // devices
+    per = hidden_total // devices
+    flat = small.reshape(devices * SMALL, 256)
+    lane = iota((128, width), 1)
+    pick = (lane % unit == iota((128, width), 0)).astype(F32).astype(BF)
+    tall = nn(flat[:, 0:128], pick)
+    row = iota((devices * SMALL, width), 0)
+    col = iota((devices * SMALL, width), 1)
+    tall = jnp.where(col // unit == row // SMALL, tall, 0.0)
+    vectors = jnp.sum(tall.reshape(devices, SMALL, width), axis=0)
+    chosen = (
+        (iota((devices, devices * SMALL), 1) == iota((devices, devices * SMALL), 0) * SMALL)
+        .astype(F32)
+        .astype(BF)
+    )
+    firsts = nn(chosen, flat[:, 128:256]).astype(BF)
+    lane = iota((128, hidden_total), 1)
+    pick = (lane % per == iota((128, hidden_total), 0)).astype(F32).astype(BF)
+    wide = nn(firsts, pick)
+    keep = iota((devices, hidden_total), 1) // per == iota((devices, hidden_total), 0)
+    return vectors, jnp.sum(jnp.where(keep, wide, 0.0), axis=0, keepdims=True)
+
+
+def gather_units(vectors, hidden_row, devices):
+    width = vectors.shape[1]
+    hidden_total = hidden_row.shape[1]
+    unit = width // devices
+    per = hidden_total // devices
+    tall = jnp.broadcast_to(vectors[None], (devices, SMALL, width)).reshape(devices * SMALL, width)
+    row = iota((devices * SMALL, width), 0)
+    col = iota((devices * SMALL, width), 1)
+    tall = jnp.where(col // unit == row // SMALL, tall, 0.0).astype(BF)
+    pick = (iota((width, 128), 0) % unit == iota((width, 128), 1)).astype(F32).astype(BF)
+    left = nn(tall, pick)
+    wide = jnp.broadcast_to(hidden_row, (devices, hidden_total))
+    keep = iota((devices, hidden_total), 1) // per == iota((devices, hidden_total), 0)
+    wide = jnp.where(keep, wide, 0.0).astype(BF)
+    pick = (iota((hidden_total, 128), 0) % per == iota((hidden_total, 128), 1)).astype(F32)
+    firsts = nn(wide, pick.astype(BF)).astype(BF)
+    chosen = (
+        iota((devices * SMALL, devices), 0) == iota((devices * SMALL, devices), 1) * SMALL
+    ).astype(F32).astype(BF)
+    right = nn(chosen, firsts)
+    return (
+        left.astype(BF).reshape(devices, SMALL, 128),
+        right.astype(BF).reshape(devices, SMALL, 128),
+    )
+
+
+def group_slice(row, j, groups):
+    width = row.shape[1] // groups
+    out = jnp.zeros((1, width), F32)
+    for g in range(groups):
+        out = jnp.where(j == g, row[:, g * width : (g + 1) * width], out)
+    return out
+
+
+def group_spread(part, j, groups):
+    return jnp.concatenate([jnp.where(j == g, part, 0.0) for g in range(groups)], axis=1)
+
+
+def block_at(place_ref, micro, position, blocks):
+    found = jnp.int32(0)
+    for s in range(blocks):
+        found = jnp.where(place_ref[0, micro, s] == position, s, found)
+    return found
+
+
+def stack_heads(rows, heads):
+    lane = iota(rows.shape, 1) // HD
+    zero = jnp.zeros_like(rows)
+    return jnp.concatenate([jnp.where(lane == h, rows, zero) for h in range(heads)], axis=0)
+
+
+def unstack_heads(tall, heads):
+    rows = tall.shape[0] // heads
+    lane = iota((rows, tall.shape[1]), 1) // HD
+    out = tall[0:rows]
+    for h in range(1, heads):
+        out = jnp.where(lane == h, tall[h * rows : (h + 1) * rows], out)
+    return out
+
+
+def visible_bias(lens, micro, start, rows, key_start, keys):
+    query = start + iota((rows, 1), 0)
+    begin = jnp.zeros((rows, 1), jnp.int32)
+    end = jnp.int32(0)
+    for s in range(lens.shape[2]):
+        end = end + lens[0, micro, s]
+        begin = jnp.where(query >= end, end, begin)
+    key = key_start + iota((rows, keys), 1)
+    return jnp.where((key >= begin) & (key <= query), 0.0, masked_score)
+
+
+def row_norm(wide):
+    average = jnp.mean(wide, axis=-1, keepdims=True)
+    centered = wide - average
+    variance = jnp.mean(centered * centered, axis=-1, keepdims=True)
+    scale = lax.rsqrt(variance + epsilon)
+    return centered * scale, scale
+
+
+def norm_back(grad, unit, scale):
+    first = jnp.mean(grad, axis=-1, keepdims=True)
+    second = jnp.mean(grad * unit, axis=-1, keepdims=True)
+    return (grad - first - unit * second) * scale
+
+
+QROWS = 128
+KCOLS = 384
+GELU_A = math.sqrt(2.0 / math.pi)
+GELU_B = 0.044715
+
+
+class Sizes:
+    def __init__(self, depth, rows, width, hidden_total):
+        self.depth = depth
+        self.rows = rows
+        self.width = width
+        self.total = depth * 8
+        self.unit = width // self.total
+        self.per = hidden_total // self.total
+        self.group = width // 4
+        self.heads = self.group // HD
+        self.pack = 8 * rows
+        self.packed = self.unit + 2 * self.per
+        self.units = self.group // self.unit
+        cut = self.per - 8
+        self.parts = (
+            (0, self.unit, "b"),
+            (self.unit, cut, "b"),
+            (self.unit + cut, 2 * self.per - cut, "a"),
+        )
+
+
+def block_scratch(n):
+    vm = lambda dims, dtype=BF: pltpu.VMEM(dims, dtype)
+    dma = lambda dims: pltpu.SemaphoreType.DMA(dims)
+    d, w, g, pack, rows = n.depth, n.width, n.group, n.pack, n.rows
+    p = len(n.parts)
+    both = 2 * rows
+    halves = 2 * d
+    chunk = n.per * 4
+    return {
+        "f_all": vm((n.total, n.packed, w)),
+        "gr": vm((d, 2, 2, 2, n.packed, w)),
+        "from_mate": vm((d, 2, 2, n.packed, w)),
+        "from_one": vm((d, 2, n.packed, w)),
+        "from_two": vm((d, n.packed, w)),
+        "from_z": vm((d, n.packed, w)),
+        "q_own": vm((3, n.unit, w)),
+        "wts": vm((3, n.units, n.unit, w)),
+        "small_all": vm((n.total, SMALL, 256)),
+        "x_all": vm((2, 2, 2, rows, w)),
+        "h": vm((pack, w)),
+        "u": vm((pack, w)),
+        "qkv": vm((3, pack, g)),
+        "o": vm((pack, -(-(g + n.heads) // 128) * 128), F32),
+        "vec": vm((SMALL, w), F32),
+        "hid": vm((halves, 1, chunk), F32),
+        "hid_grad": vm((halves, 1, chunk), F32),
+        "stage": vm((8, rows, g)),
+        "at_recv": vm((8, rows, g)),
+        "da_recv": vm((8, rows, g)),
+        "resid": vm((both, w), F32),
+        "unit2": vm((both, w), F32),
+        "h2": vm((both, w)),
+        "scale2": vm((both, 1), F32),
+        "vec_grad": vm((SMALL, w), F32),
+        "da": vm((pack, g)),
+        "dk_acc": vm((pack, g), F32),
+        "dv_acc": vm((pack, g), F32),
+        "gq": vm((3, n.units // 2, 2, n.unit, w)),
+        "q_mate": vm((3, n.units // 2, n.unit, w)),
+        "q_line": vm((3, d, n.unit, w)),
+        "dh_a1": vm((2, rows, w)),
+        "dh_b1": vm((2, rows, w)),
+        "dh_a2": vm((rows, w)),
+        "dh_b2": vm((rows, w)),
+        "dh_mate": vm((rows, w)),
+        "sums": vm((SMALL, w), F32),
+        "sg": vm((n.total, SMALL, 256)),
+        "sg_recv": vm((n.total, SMALL, 256)),
+        "s_zsend": dma((p, d)),
+        "s_zrecv": dma((p, d)),
+        "s_send1": dma((p, d)),
+        "s_recv1": dma((p, d)),
+        "s_send2": dma((p, d, 2)),
+        "s_recv2": dma((p, d, 2)),
+        "s_csend": dma((p, d, 4)),
+        "s_crecv": dma((p, d, 4)),
+        "s_xsend": dma((7,)),
+        "s_xrecv": dma((8,)),
+        "s_qsend": dma((3, d)),
+        "s_qrecv": dma((3, n.units)),
+        "s_qcsend": dma((3, n.units)),
+        "s_smsend": dma((n.total,)),
+        "s_smrecv": dma((n.total,)),
+        "s_asend": dma((8,)),
+        "s_arecv": dma((8,)),
+        "s_dsend": dma((8,)),
+        "s_drecv": dma((8,)),
+        "s_rcs": dma((p, d)),
+        "s_rcr": dma((p, d)),
+        "s_r1s": dma((p, d)),
+        "s_r1r": dma((p, d)),
+        "s_r2s": dma((p, d)),
+        "s_r2r": dma((p, d)),
+        "s_rzs": dma((p, d)),
+        "s_rzr": dma((p, d)),
+        "s_gqc": dma((2,)),
+        "s_gqs": dma((3, n.units // 2)),
+        "s_gqr": dma((3, d)),
+        "s_dhs": dma((5,)),
+        "s_dhr": dma((5,)),
+        "s_sgs": dma((n.total,)),
+        "s_sgr": dma((n.total,)),
+    }
+
+
+def add_into(target, source):
+    target[...] = (target[...].astype(F32) + source[...].astype(F32)).astype(BF)
+
+
+def block_kernel(n, names, tie, lens, spans, x_ref, dy_ref, *refs):
+    banks = refs[:13]
+    y_out, dr_out, dh_out, f_sum, q_sum, small_sum, vec_out = refs[13:20]
+    s = types.SimpleNamespace(**dict(zip(names, refs[20:])))
+    g1, s1, wq, bq, bv, wo, bo, g2, s2, wu, bu, wd, bd = banks
+    depth, unit, per, rows, width, group, heads = (
+        n.depth, n.unit, n.per, n.rows, n.width, n.group, n.heads
+    )
+    here = Place(depth)
+    z, r, a, b, core, j = here.z, here.r, here.a, here.b, here.core, here.j
+    me = here.slot(z, r)
+    micro = core
+    mate, by_a, by_b, both = here.mate, here.by_a, here.by_b, here.both
+    parts = n.parts
+    main = (1, 2)
+    groups = 4
+
+    bar = pltpu.get_barrier_semaphore()
+
+    def signal(k, carry):
+        other = (me + k) % n.total
+        pl.semaphore_signal(bar, inc=1, device_id=(other // 8, other % 8), device_id_type=MESH)
+        return carry
+
+    lax.fori_loop(1, n.total, signal, 0)
+
+    f_own = s.f_all.at[me]
+    f_own[0:unit, :] = wo[tie[5]]
+    f_own[unit : unit + per, :] = wu[tie[9]]
+    f_own[unit + per :, :] = wd[tie[11]]
+    s.q_own[...] = wq[tie[2]].reshape(3, unit, width)
+    chosen_rows = []
+    for bank, index in ((g1, 0), (s1, 1), (bq, 3), (bv, 4), (bo, 6), (g2, 7), (s2, 8), (bd, 12)):
+        wide = bank[...].astype(F32)
+        chosen = jnp.zeros((1, unit), F32)
+        for layer in range(bank.shape[0]):
+            chosen = jnp.where(tie[index] == layer, wide[layer : layer + 1, :], chosen)
+        chosen_rows.append(chosen)
+    small_own = s.small_all.at[me]
+    small_own[...] = jnp.zeros((SMALL, 256), BF)
+    small_own[:, 0:unit] = jnp.concatenate(chosen_rows, axis=0).astype(BF)
+    wide = bu[...].astype(F32)
+    chosen = jnp.zeros((1, per), F32)
+    for layer in range(bu.shape[0]):
+        chosen = jnp.where(tie[10] == layer, wide[layer : layer + 1, :], chosen)
+    tall = jnp.concatenate([chosen, jnp.zeros((SMALL - 1, per), F32)], axis=0)
+    small_own[:, 128 : 128 + per] = tall.astype(BF)
+
+    pl.semaphore_wait(bar, n.total - 1)
+
+    def to_all(buffer_of, send, recv, target):
+        def go(k, carry):
+            other = (me + k) % n.total
+            remote(
+                buffer_of(other), target.at[me], send.at[other], recv.at[me], other // 8, other % 8
+            ).start()
+            return carry
+
+        lax.fori_loop(1, n.total, go, 0)
+
+    def from_all(buffer, send, recv, target):
+        def go(k, carry):
+            other = (me + k) % n.total
+            remote(
+                buffer, target.at[other], send.at[other], recv.at[other], other // 8, other % 8
+            ).wait()
+            return carry
+
+        lax.fori_loop(1, n.total, go, 0)
+
+    def row_block(block):
+        return s.x_all.at[block // 4, (block // 2) % 2, block % 2]
+
+    def row_move(source, block, lane, to):
+        return remote(source, row_block(block), s.s_xsend.at[lane], s.s_xrecv.at[block], z, to)
+
+    mate_a = by_a + 1 - 2 * core
+    row_move(x_ref.at[1 - core], r, 0, mate).start()
+    row_move(x_ref.at[core], r, 1, by_b).start()
+    row_move(x_ref.at[core], r, 2, by_a).start()
+    to_all(lambda other: small_own, s.s_smsend, s.s_smrecv, s.small_all)
+    row_block(r)[...] = x_ref[core]
+
+    def q_unit(t):
+        block = me * 3 + t
+        kind = block // n.total
+        inside = block % n.total
+        return kind, inside // n.units, inside % n.units
+
+    def q_first(t, zz):
+        kind, chip, at = q_unit(t)
+        to = chip * 2 + core
+        source, target, recv = s.q_own.at[t], s.wts.at[kind, at], s.s_qrecv.at[kind, at]
+        go = lambda: remote(source, target, s.s_qsend.at[t, zz], recv, zz, to)
+        stay = lambda: pltpu.make_async_copy(source, target, recv)
+        return go, stay, (zz == z) & (to == r)
+
+    for t in range(3):
+        for zz in range(depth):
+            go, stay, mine = q_first(t, zz)
+
+            @pl.when(jnp.logical_not(mine))
+            def _():
+                go().start()
+
+            @pl.when(mine)
+            def _():
+                stay().start()
+
+    def order(k):
+        out = jnp.int32(0)
+        for zz in range(depth):
+            line = sorted(range(depth), key=lambda t: (abs(t - zz), t))
+            for kk in range(depth):
+                out = jnp.where((z == zz) & (k == kk), line[kk], out)
+        return out
+
+    def move(p, zz, rr, send, recv, to_z, to_r):
+        start, count, _ = parts[p]
+        ref = s.f_all.at[here.slot(zz, rr), pl.ds(start, count)]
+        return remote(ref, ref, send, recv, to_z, to_r)
+
+    def first_axis(p):
+        return by_b if parts[p][2] == "b" else by_a
+
+    def second_axis(p):
+        return by_a if parts[p][2] == "b" else by_b
+
+    def line_move(p, o, to_z):
+        return move(p, o, r, s.s_zsend.at[p, to_z], s.s_zrecv.at[p, o], to_z, r)
+
+    def one(p, o):
+        return move(p, o, r, s.s_send1.at[p, o], s.s_recv1.at[p, o], z, first_axis(p))
+
+    def two(p, o, rr, lane):
+        return move(
+            p, o, rr, s.s_send2.at[p, o, lane], s.s_recv2.at[p, o, lane], z, second_axis(p)
+        )
+
+    def across(p, o, rr, lane):
+        return move(p, o, rr, s.s_csend.at[p, o, lane], s.s_crecv.at[p, o, lane], z, mate)
+
+    every = range(len(parts))
+    for p in every:
+        for k in range(1, depth):
+            line_move(p, z, order(k)).start()
+
+    def row_arrived(block):
+        row_move(x_ref.at[0], block, 0, mate).wait_recv()
+
+    row_arrived(mate)
+    row_move(row_block(mate), mate, 3, by_a).start()
+    row_move(row_block(mate), mate, 4, by_b).start()
+    row_arrived(by_b)
+    row_move(row_block(by_b), by_b, 5, by_a).start()
+    row_arrived(mate_a)
+    row_move(row_block(mate_a), mate_a, 6, by_b).start()
+
+    def q_relay(e, carry):
+        kind, at = e // n.units, e % n.units
+        owner = (kind * n.total + j * n.units + at) // 3
+        unit_ref = s.wts.at[kind, at]
+
+        @pl.when(owner % 2 == core)
+        def _():
+            pltpu.make_async_copy(unit_ref, unit_ref, s.s_qrecv.at[kind, at]).wait()
+            remote(
+                unit_ref, unit_ref, s.s_qcsend.at[kind, at], s.s_qrecv.at[kind, at], z, mate
+            ).start()
+
+        return carry
+
+    lax.fori_loop(0, 3 * n.units, q_relay, 0)
+
+    def spread_own(p):
+        one(p, z).start()
+        two(p, z, r, 0).start()
+        across(p, z, r, 0).start()
+
+    for p in every:
+        spread_own(p)
+
+    from_all(small_own, s.s_smsend, s.s_smrecv, s.small_all)
+    vectors, hidden = spread_units(s.small_all[...], width, per * n.total)
+    s.vec[...] = vectors
+    vec_out[...] = vectors
+    chunk = 4 * per
+    for c in range(2 * depth):
+        s.hid[c] = hidden[:, c * chunk : (c + 1) * chunk]
+
+    row_arrived(by_a)
+    row_arrived(both)
+    row_arrived(by_b + 1 - 2 * core)
+    row_arrived(both + 1 - 2 * core)
+
+    def q_rest(e, carry):
+        kind, at = e // n.units, e % n.units
+        owner = (kind * n.total + j * n.units + at) // 3
+        unit_ref = s.wts.at[kind, at]
+
+        @pl.when(owner % 2 != core)
+        def _():
+            remote(
+                unit_ref, unit_ref, s.s_qcsend.at[kind, at], s.s_qrecv.at[kind, at], z, mate
+            ).wait_recv()
+
+        return carry
+
+    lax.fori_loop(0, 3 * n.units, q_rest, 0)
+
+    gain, shift = s.vec[0:1, :], s.vec[1:2, :]
+    query_add = group_slice(s.vec[2:3, :], j, groups)
+    value_add = group_slice(s.vec[3:4, :], j, groups)
+
+    def weight(kind):
+        return s.wts[kind].reshape(group, width)
+
+    def project(p, carry):
+        source = block_at(spans, micro, p, 8)
+        unit_rows, _ = row_norm(
+            s.x_all[source // 4, (source // 2) % 2, source % 2].astype(F32)
+        )
+        normed = (unit_rows * gain + shift).astype(BF)
+        at = pl.ds(pl.multiple_of(p * rows, 16), rows)
+        s.u[at, :] = unit_rows.astype(BF)
+        s.h[at, :] = normed
+        s.qkv[0, at, :] = (nt(normed, weight(0)) + query_add).astype(BF)
+        s.qkv[1, at, :] = nt(normed, weight(1)).astype(BF)
+        s.qkv[2, at, :] = (nt(normed, weight(2)) + value_add).astype(BF)
+        return carry
+
+    lax.fori_loop(0, 8, project, 0)
+
+    def line_event(k, which):
+        o = order(k)
+        for p in which:
+            line_move(p, o, z).wait_recv()
+            one(p, o).start()
+            two(p, o, r, 0).start()
+            across(p, o, r, 0).start()
+
+    def first_event(k, which):
+        o = order(k)
+        for p in which:
+            one(p, o).wait_recv()
+            two(p, o, first_axis(p), 1).start()
+            across(p, o, first_axis(p), 1).start()
+
+    def second_event(o, which):
+        for p in which:
+            two(p, o, r, 0).wait_recv()
+            across(p, o, second_axis(p), 2).start()
+            two(p, o, r, 1).wait_recv()
+            across(p, o, both, 3).start()
+
+    def all_here(o, which):
+        for p in which:
+            for lane in range(4):
+                across(p, o, r, lane).wait_recv()
+
+    gather_events = {
+        0: [lambda: line_event(1, (0,)), lambda: line_event(1, main)],
+        1: [lambda: line_event(2, (0,)), lambda: first_event(0, (0,))],
+        2: [lambda: line_event(3, (0,)), lambda: first_event(0, main)],
+        3: [lambda: line_event(2, main)],
+        4: [lambda: first_event(1, (0,)), lambda: first_event(1, main)],
+        5: [lambda: first_event(2, (0,))],
+        6: [lambda: line_event(3, main), lambda: first_event(3, (0,))],
+        7: [lambda: first_event(2, main)],
+        8: [lambda: first_event(3, main)],
+    }
+
+    def run_events(events, i):
+        for at, acts in events.items():
+
+            @pl.when(i == at)
+            def _(acts=acts):
+                for act in acts:
+                    act()
+
+    tall = heads * QROWS
+    q_blocks = n.pack // QROWS
+
+    def attend(i, carry):
+        start = pl.multiple_of(i * QROWS, QROWS)
+        stacked = stack_heads(s.qkv[0, pl.ds(start, QROWS), :] * BF(score_scale), heads)
+
+        def step(kc, state):
+            top, total, acc = state
+            at = pl.ds(pl.multiple_of(kc * KCOLS, KCOLS), KCOLS)
+            bias = visible_bias(lens, micro, start, QROWS, kc * KCOLS, KCOLS)
+            scores = nt(stacked, s.qkv[1, at, :])
+            scores = (scores.reshape(heads, QROWS, KCOLS) + bias[None]).reshape(tall, KCOLS)
+            new_top = jnp.maximum(top, jnp.max(scores, axis=1, keepdims=True))
+            probs = jnp.exp(scores - new_top)
+            factor = jnp.exp(top - new_top)
+            total = total * factor + jnp.sum(probs, axis=1, keepdims=True)
+            acc = acc * factor + nn(probs.astype(BF), s.qkv[2, at, :])
+            return new_top, total, acc
+
+        top, total, acc = lax.fori_loop(
+            0,
+            (i * QROWS) // KCOLS + 1,
+            step,
+            (
+                jnp.full((tall, 1), masked_score, F32),
+                jnp.zeros((tall, 1), F32),
+                jnp.zeros((tall, group), F32),
+            ),
+        )
+        at_q = pl.ds(start, QROWS)
+        s.o[at_q, 0:group] = unstack_heads(acc / total, heads)
+        lse = top + jnp.log(total)
+        for head in range(heads):
+            s.o[at_q, group + head : group + head + 1] = lse[head * QROWS : (head + 1) * QROWS]
+        run_events(gather_events, i)
+        return carry
+
+    lax.fori_loop(0, q_blocks, attend, 0)
+
+    for e in range(8):
+        at = pl.ds(spans[0, micro, e] * rows, rows)
+        s.stage[e] = s.o[at, 0:group].astype(BF)
+
+    def exchange_start(stage, target, send, recv):
+        for k in range(1, 8):
+            to = (r + k) % 8
+            remote(stage.at[to], target.at[r], send.at[to], recv.at[r], z, to).start()
+        target[r] = stage[r]
+
+    def exchange_wait(stage, target, send, recv):
+        for k in range(1, 8):
+            frm = (r + k) % 8
+            remote(stage.at[frm], target.at[frm], send.at[frm], recv.at[frm], z, frm).wait()
+
+    exchange_start(s.stage, s.at_recv, s.s_asend, s.s_arecv)
+    for k in range(depth):
+        second_event(order(k), (0,))
+    second_event(z, main)
+    for k in range(depth):
+        all_here(order(k), (0,))
+    exchange_wait(s.stage, s.at_recv, s.s_asend, s.s_arecv)
+
+    full = 2 * rows
+    def attended():
+        pieces = [
+            jnp.concatenate([s.at_recv[2 * g], s.at_recv[2 * g + 1]], axis=0)
+            for g in range(groups)
+        ]
+        return jnp.concatenate(pieces, axis=1)
+
+    out_w = s.f_all[:, 0:unit, :].reshape(width, width)
+    res = (
+        x_ref[...].reshape(full, width).astype(F32) + nt(attended(), out_w) + s.vec[4:5, :]
+    )
+    s.resid[...] = res + s.vec[7:8, :]
+    unit_rows, scale = row_norm(res)
+    s.unit2[...] = unit_rows
+    s.scale2[...] = scale
+    s.h2[...] = (unit_rows * s.vec[5:6, :] + s.vec[6:7, :]).astype(BF)
+    dr_out[...] = jnp.zeros_like(dr_out)
+
+    def cut(p):
+        return pl.ds(parts[p][0], parts[p][1])
+
+    def sum_mate(p, t):
+        return remote(
+            s.gr.at[t, :, :, 1 - core, cut(p)],
+            s.from_mate.at[t, :, :, cut(p)],
+            s.s_rcs.at[p, t],
+            s.s_rcr.at[p, t],
+            z,
+            mate,
+        )
+
+    def sum_first(p, t):
+        if parts[p][2] == "b":
+            source, to = s.gr.at[t, 1 - a, :, core, cut(p)], by_a
+        else:
+            source, to = s.gr.at[t, :, 1 - b, core, cut(p)], by_b
+        target = s.from_one.at[t, :, cut(p)]
+        return remote(source, target, s.s_r1s.at[p, t], s.s_r1r.at[p, t], z, to)
+
+    def sum_second(p, t):
+        if parts[p][2] == "b":
+            source, to = s.gr.at[t, a, 1 - b, core, cut(p)], by_b
+        else:
+            source, to = s.gr.at[t, 1 - a, b, core, cut(p)], by_a
+        target = s.from_two.at[t, cut(p)]
+        return remote(source, target, s.s_r2s.at[p, t], s.s_r2r.at[p, t], z, to)
+
+    def sum_line(p, t, origin):
+        return remote(
+            s.gr.at[t, a, b, core, cut(p)],
+            s.from_z.at[origin, cut(p)],
+            s.s_rzs.at[p, t],
+            s.s_rzr.at[p, origin],
+            t,
+            r,
+        )
+
+    def start_sum(t, which):
+        for p in which:
+            sum_mate(p, t).start()
+
+    def event_one(t, which):
+        for p in which:
+            sum_mate(p, t).wait_recv()
+            for aa in range(2):
+                for bb in range(2):
+                    add_into(s.gr.at[t, aa, bb, core, cut(p)], s.from_mate.at[t, aa, bb, cut(p)])
+            sum_first(p, t).start()
+
+    def event_two(t, which):
+        for p in which:
+            sum_first(p, t).wait_recv()
+            for e in range(2):
+                mine = (
+                    s.gr.at[t, a, e, core, cut(p)]
+                    if parts[p][2] == "b"
+                    else s.gr.at[t, e, b, core, cut(p)]
+                )
+                add_into(mine, s.from_one.at[t, e, cut(p)])
+            sum_second(p, t).start()
+
+    def event_three(t, which):
+        for p in which:
+            sum_second(p, t).wait_recv()
+            add_into(s.gr.at[t, a, b, core, cut(p)], s.from_two.at[t, cut(p)])
+
+            @pl.when(t != z)
+            def _(p=p):
+                sum_line(p, t, z).start()
+
+    g_down = dy_ref[...].reshape(full, width)
+
+    def feed(c, carry):
+        k, half = c // 2, c % 2
+        o = order(k)
+
+        @pl.when((half == 0) & (k > 0))
+        def _():
+            second_event(o, main)
+
+        @pl.when(half == 0)
+        def _():
+            all_here(o, main)
+
+        devices = pl.ds(o * 8 + half * 4, 4)
+        up_w = s.f_all[devices, unit : unit + per, :].reshape(chunk, width)
+        down_w = s.f_all[devices, unit + per : unit + 2 * per, :].reshape(chunk, width)
+        where = o * 2 + half
+        up = nt(s.h2[...], up_w) + s.hid[where]
+        square = up * up
+        tanh = jnp.tanh(GELU_A * (up + GELU_B * square * up))
+        side = 0.5 * (1.0 + tanh)
+        act = (up * side).astype(BF)
+        s.resid[...] += nn(act, down_w)
+        slope = side + 0.5 * up * (1.0 - tanh * tanh) * (GELU_A * (1.0 + 3.0 * GELU_B * square))
+        grad = dy_ref[...].reshape(full, width)
+        d_up = (nt(grad, down_w) * slope).astype(BF)
+        s.hid_grad[where] = jnp.sum(d_up.astype(F32), axis=0, keepdims=True)
+        dr_out[...] += nn(d_up, up_w).reshape(2, rows, width)
+        s.gr[o, half, :, :, unit : unit + per, :] = (
+            tn(d_up, s.h2[...]).astype(BF).reshape(2, 2, per, width)
+        )
+        s.gr[o, half, :, :, unit + per : unit + 2 * per, :] = (
+            tn(act, grad).astype(BF).reshape(2, 2, per, width)
+        )
+
+        @pl.when(half == 1)
+        def _():
+            start_sum(o, main)
+
+            @pl.when(k > 0)
+            def _():
+                event_one(order(k - 1), main)
+
+        return carry
+
+    lax.fori_loop(0, 2 * depth, feed, 0)
+
+    dy = g_down.astype(F32)
+    y_out[...] = s.resid[...].astype(BF).reshape(2, rows, width)
+    d_h2 = dr_out[...].reshape(full, width)
+    unit_rows = s.unit2[...]
+    d_res = dy + norm_back(d_h2 * s.vec[5:6, :], unit_rows, s.scale2[...])
+    dr_out[...] = d_res.reshape(2, rows, width)
+    g_mix = d_res.astype(BF)
+    d_attn = nn(g_mix, s.f_all[:, 0:unit, :].reshape(width, width)).astype(BF)
+    for m in range(2):
+        for g in range(groups):
+            s.stage[2 * g + m] = d_attn[
+                m * rows : (m + 1) * rows, g * group : (g + 1) * group
+            ]
+    exchange_start(s.stage, s.da_recv, s.s_dsend, s.s_drecv)
+    out_grad = tn(g_mix, attended()).astype(BF).reshape(depth, 2, 2, 2, unit, width)
+    s.gr[:, :, :, :, 0:unit, :] = out_grad
+    for k in range(depth):
+        start_sum(order(k), (0,))
+    s.vec_grad[...] = jnp.zeros_like(s.vec_grad)
+    s.vec_grad[4:5, :] = jnp.sum(g_mix.astype(F32), axis=0, keepdims=True)
+    s.vec_grad[5:6, :] = jnp.sum(d_h2 * unit_rows, axis=0, keepdims=True)
+    s.vec_grad[6:7, :] = jnp.sum(d_h2, axis=0, keepdims=True)
+    s.vec_grad[7:8, :] = jnp.sum(dy, axis=0, keepdims=True)
+    event_one(order(depth - 1), main)
+    exchange_wait(s.stage, s.da_recv, s.s_dsend, s.s_drecv)
+
+    for p in range(8):
+        s.da[p * rows : (p + 1) * rows, :] = s.da_recv[block_at(spans, micro, p, 8)]
+    s.dk_acc[...] = jnp.zeros_like(s.dk_acc)
+    s.dv_acc[...] = jnp.zeros_like(s.dv_acc)
+
+    def out_events(act):
+        def go():
+            for k in range(depth):
+                act(order(k), (0,))
+
+        return go
+
+    sum_events = {
+        0: [lambda: event_two(order(0), main)],
+        1: [lambda: event_two(order(1), main)],
+        2: [lambda: event_two(order(2), main), lambda: event_three(order(0), main)],
+        3: [out_events(event_one), lambda: event_three(order(1), main)],
+        4: [lambda: event_two(order(3), main)],
+        5: [out_events(event_two), lambda: event_three(order(2), main)],
+        6: [lambda: event_three(order(3), main)],
+        8: [out_events(event_three)],
+    }
+
+    def query_block(i, carry):
+        start = pl.multiple_of(i * QROWS, QROWS)
+        at_q = pl.ds(start, QROWS)
+        stacked = stack_heads(s.qkv[0, at_q, :] * BF(score_scale), heads)
+        d_rows = s.da[at_q, :]
+        d_stacked = stack_heads(d_rows, heads)
+        product = d_rows.astype(F32) * s.o[at_q, 0:group]
+        delta = jnp.sum(stack_heads(product, heads), axis=1, keepdims=True)
+        lse = jnp.concatenate(
+            [s.o[at_q, group + head : group + head + 1] for head in range(heads)], axis=0
+        )
+
+        def step(kc, acc):
+            at = pl.ds(pl.multiple_of(kc * KCOLS, KCOLS), KCOLS)
+            bias = visible_bias(lens, micro, start, QROWS, kc * KCOLS, KCOLS)
+            keys = s.qkv[1, at, :]
+            scores = nt(stacked, keys)
+            scores = (scores.reshape(heads, QROWS, KCOLS) + bias[None]).reshape(tall, KCOLS)
+            probs = jnp.exp(scores - lse)
+            d_probs = nt(d_stacked, s.qkv[2, at, :])
+            d_scores = (probs * (d_probs - delta)).astype(BF)
+            s.dk_acc[at, :] += tn(d_scores, stacked)
+            s.dv_acc[at, :] += tn(probs.astype(BF), d_stacked)
+            return acc + nn(d_scores, keys)
+
+        acc = lax.fori_loop(0, (i * QROWS) // KCOLS + 1, step, jnp.zeros((tall, group), F32))
+        s.qkv[0, at_q, :] = (unstack_heads(acc, heads) * score_scale).astype(BF)
+        run_events(sum_events, i)
+        return carry
+
+    lax.fori_loop(0, q_blocks, query_block, 0)
+    s.qkv[1] = s.dk_acc[...].astype(BF)
+    s.qkv[2] = s.dv_acc[...].astype(BF)
+
+    pairs = n.units // 2
+    for kind in range(3):
+        s.gq[kind] = tn(s.qkv[kind], s.h[...]).astype(BF).reshape(pairs, 2, unit, width)
+    q_mate = remote(
+        s.gq.at[:, :, 1 - core], s.q_mate, s.s_gqc.at[0], s.s_gqc.at[1], z, mate
+    )
+    q_mate.start()
+
+    def q_route(kind, m):
+        block = kind * n.total + j * n.units + m * 2 + core
+        owner = block // 3
+        return owner // 8, owner % 8, block % 3
+
+    def q_out(kind, m):
+        oz, orr, at = q_route(kind, m)
+        source = s.gq.at[kind, m, core]
+        target, send = s.q_line.at[at, z], s.s_gqs.at[kind, m]
+        go = lambda: remote(source, target, send, s.s_gqr.at[at, z], oz, orr)
+        stay = lambda: pltpu.make_async_copy(source, target, send)
+        return go, stay, (oz == z) & (orr == r)
+
+    def q_sums(act):
+        def each(e, carry):
+            kind, m = e // pairs, e % pairs
+            go, stay, mine = q_out(kind, m)
+            act(kind, m, go, stay, mine)
+            return carry
+
+        lax.fori_loop(0, 3 * pairs, each, 0)
+
+    def q_send(kind, m, go, stay, mine):
+        add_into(s.gq.at[kind, m, core], s.q_mate.at[kind, m])
+
+        @pl.when(jnp.logical_not(mine))
+        def _():
+            go().start()
+
+        @pl.when(mine)
+        def _():
+            stay().start()
+
+    def q_sent(kind, m, go, stay, mine):
+        @pl.when(jnp.logical_not(mine))
+        def _():
+            go().wait_send()
+
+        @pl.when(mine)
+        def _():
+            stay().wait()
+
+    for lane in range(7):
+        row_move(x_ref.at[0], r, lane, mate).wait_send()
+    s.sums[...] = jnp.zeros_like(s.sums)
+
+    def dh_a1():
+        return remote(s.x_all.at[1 - a, :, core], s.dh_a1, s.s_dhs.at[0], s.s_dhr.at[0], z, by_a)
+
+    def dh_b1():
+        return remote(s.x_all.at[:, 1 - b, 1 - core], s.dh_b1, s.s_dhs.at[1], s.s_dhr.at[1], z, by_b)
+
+    def dh_a2():
+        return remote(s.x_all.at[a, 1 - b, core], s.dh_a2, s.s_dhs.at[2], s.s_dhr.at[2], z, by_b)
+
+    def dh_b2():
+        return remote(s.x_all.at[1 - a, b, 1 - core], s.dh_b2, s.s_dhs.at[3], s.s_dhr.at[3], z, by_a)
+
+    def dh_m():
+        return remote(s.x_all.at[a, b, 1 - core], s.dh_mate, s.s_dhs.at[4], s.s_dhr.at[4], z, mate)
+
+    def unsort(e, carry):
+        late, kind, lane = e // 4, (e % 4) // 2, e % 2
+        aa = jnp.where(kind == 0, jnp.where(late == 1, a, 1 - a), lane)
+        bb = jnp.where(kind == 0, lane, jnp.where(late == 1, b, 1 - b))
+        cc = jnp.where(kind == 0, core, 1 - core)
+        at = pl.ds(spans[0, micro, aa * 4 + bb * 2 + cc] * rows, rows)
+        part = (
+            nn(s.qkv[0, at, :], weight(0))
+            + nn(s.qkv[1, at, :], weight(1))
+            + nn(s.qkv[2, at, :], weight(2))
+        )
+        s.x_all[aa, bb, cc] = part.astype(BF)
+        s.sums[0:1, :] += jnp.sum(part * s.u[at, :].astype(F32), axis=0, keepdims=True)
+        s.sums[1:2, :] += jnp.sum(part, axis=0, keepdims=True)
+
+        @pl.when(e == 3)
+        def _():
+            dh_a1().start()
+            dh_b1().start()
+            q_mate.wait_recv()
+            q_sums(q_send)
+
+        return carry
+
+    lax.fori_loop(0, 8, unsort, 0)
+
+    query_bias = jnp.sum(s.qkv[0].astype(F32), axis=0, keepdims=True)
+    value_bias = jnp.sum(s.qkv[2].astype(F32), axis=0, keepdims=True)
+    s.vec_grad[0:2, :] = s.sums[0:2, :]
+    s.vec_grad[2:3, :] = group_spread(query_bias, j, groups)
+    s.vec_grad[3:4, :] = group_spread(value_bias, j, groups)
+    hidden_row = jnp.concatenate([s.hid_grad[c] for c in range(2 * depth)], axis=1)
+    left, right = gather_units(s.vec_grad[...], hidden_row, n.total)
+    s.sg[:, :, 0:128] = left
+    s.sg[:, :, 128:256] = right
+    to_all(lambda other: s.sg.at[other], s.s_sgs, s.s_sgr, s.sg_recv)
+    s.sg_recv[me] = s.sg[me]
+
+    dh_a1().wait_recv()
+    for e in range(2):
+        add_into(s.x_all.at[a, e, core], s.dh_a1.at[e])
+    dh_a2().start()
+    dh_b1().wait_recv()
+    for e in range(2):
+        add_into(s.x_all.at[e, b, 1 - core], s.dh_b1.at[e])
+    dh_b2().start()
+    dh_b2().wait_recv()
+    add_into(s.x_all.at[a, b, 1 - core], s.dh_b2)
+    dh_m().start()
+
+    for k in range(1, depth):
+        o = order(k)
+        for p in every:
+            sum_line(p, z, o).wait_recv()
+    total_rows = s.gr[z, a, b, core].astype(F32)
+    for k in range(1, depth):
+        total_rows = total_rows + s.from_z[order(k)].astype(F32)
+    f_sum[...] = total_rows
+
+    dh_a2().wait_recv()
+    dh_out[core] = s.x_all[a, b, core].astype(F32) + s.dh_a2[...].astype(F32)
+    dh_m().wait_recv()
+    dh_out[1 - core] = s.dh_mate[...].astype(F32)
+
+    from_all(s.sg.at[0], s.s_sgs, s.s_sgr, s.sg_recv)
+    small_sum[...] = jnp.sum(s.sg_recv[...].astype(F32), axis=0)
+
+    def q_arrivals(at, zz):
+        block = me * 3 + at
+        inside = block % n.total
+        from_r = (inside // n.units) * 2 + (inside % n.units) % 2
+        ref = s.q_line.at[at, zz]
+        come = lambda: remote(ref, ref, s.s_gqs.at[0, 0], s.s_gqr.at[at, zz], zz, from_r)
+        return come, (from_r == r) & (zz == z)
+
+    for at in range(3):
+        for zz in range(depth):
+            come, mine = q_arrivals(at, zz)
+
+            @pl.when(jnp.logical_not(mine))
+            def _():
+                come().wait_recv()
+
+    q_sums(q_sent)
+    for at in range(3):
+        part = s.q_line[at, 0].astype(F32)
+        for zz in range(1, depth):
+            part = part + s.q_line[at, zz].astype(F32)
+        q_sum[at] = part
+
+    for t in range(3):
+        for zz in range(depth):
+            go, _, mine = q_first(t, zz)
+
+            @pl.when(jnp.logical_not(mine))
+            def _():
+                go().wait_send()
+
+    def q_relayed(e, carry):
+        kind, at = e // n.units, e % n.units
+        owner = (kind * n.total + j * n.units + at) // 3
+        unit_ref = s.wts.at[kind, at]
+
+        @pl.when(owner % 2 == core)
+        def _():
+            remote(
+                unit_ref, unit_ref, s.s_qcsend.at[kind, at], s.s_qrecv.at[kind, at], z, mate
+            ).wait_send()
+
+        return carry
+
+    lax.fori_loop(0, 3 * n.units, q_relayed, 0)
+    q_mate.wait_send()
+    for act in (dh_a1, dh_b1, dh_a2, dh_b2, dh_m):
+        act().wait_send()
+
+    def drain(o, carry):
+        for p in every:
+            one(p, o).wait_send()
+            for lane in range(2):
+                two(p, o, r, lane).wait_send()
+            for lane in range(4):
+                across(p, o, r, lane).wait_send()
+            sum_mate(p, o).wait_send()
+            sum_first(p, o).wait_send()
+            sum_second(p, o).wait_send()
+
+            @pl.when(o != z)
+            def _(p=p):
+                line_move(p, z, o).wait_send()
+                sum_line(p, o, z).wait_send()
+
+        return carry
+
+    lax.fori_loop(0, depth, drain, 0)
+
+
+def run_block(n, tie_map, lens, spans, x_own, dy_own, banks):
+    rows, width = n.rows, n.width
+    scratch = block_scratch(n)
+    outs = (
+        shape((2, rows, width), BF),
+        shape((2, rows, width), F32),
+        shape((2, rows, width), F32),
+        shape((n.packed, width), F32),
+        shape((3, n.unit, width), F32),
+        shape((SMALL, 256), F32),
+        shape((SMALL, width), F32),
+    )
+    return pl.pallas_call(
+        functools.partial(block_kernel, n, tuple(scratch)),
+        name="block",
+        out_shape=outs,
+        in_specs=[smem()] * 3 + [vmem()] * 15,
+        out_specs=(vmem(),) * len(outs),
+        scratch_shapes=list(scratch.values()),
+        compiler_params=params(1),
+    )(tie_map, lens, spans, x_own, dy_own, *banks)
+
+
+def final_kernel(
+    n, tie, x_ref, y_ref, dh_ref, dr_ref, vec_ref, f_ref, q_ref, small_ref, y_out, dx_out, *grads
+):
+    g1, s1, wq, bq, bv, wo, bo, g2, s2, wu, bu, wd, bd = grads
+    y_out[...] = y_ref[...]
+    for m in range(x_ref.shape[0]):
+        unit_rows, scale = row_norm(x_ref[m].astype(F32))
+        back = norm_back(dh_ref[m] * vec_ref[0:1, :], unit_rows, scale)
+        dx_out[m] = (dr_ref[m] + back).astype(BF)
+    layers = wq.shape[0]
+    unit, per = n.unit, n.per
+
+    def put(ref, index, value):
+        for layer in range(layers):
+            ref[layer] = jnp.where(tie[index] == layer, value, 0.0)
+
+    put(wo, 5, f_ref[0:unit, :])
+    put(wu, 9, f_ref[unit : unit + per, :])
+    put(wd, 11, f_ref[unit + per :, :])
+    put(wq, 2, q_ref[...].reshape(3 * unit, n.width))
+    names = ((g1, 0), (s1, 1), (bq, 3), (bv, 4), (bo, 6), (g2, 7), (s2, 8), (bd, 12))
+    for e, (ref, index) in enumerate(names):
+        for layer in range(layers):
+            ref[layer : layer + 1, :] = jnp.where(
+                tie[index] == layer, small_ref[e : e + 1, 0:unit], 0.0
+            )
+    for layer in range(layers):
+        bu[layer : layer + 1, :] = jnp.where(
+            tie[10] == layer, small_ref[0:1, 128 : 128 + per], 0.0
+        )
+
+
+def turned(bank):
+    return jnp.swapaxes(bank, 1, 2)
+
+
+def grouped_plan(depth, *args):
+    block_input, cotangent, tie_map, seq_lengths, span_place = args[:5]
+    banks = list(args[5:])
+    for index in (2, 5, 9):
+        banks[index] = turned(banks[index])
+    x_own, dy_own = block_input[0], cotangent[0]
+    n = Sizes(depth, x_own.shape[1], x_own.shape[2], banks[10].shape[1] * depth * 8)
+    y, d_resid, dh, f_sum, q_sum, small_sum, vectors = run_block(
+        n, tie_map, seq_lengths, span_place, x_own, dy_own, banks
+    )
+    outs = (shape(x_own.shape, BF),) * 2 + tuple(shape(bank.shape, F32) for bank in banks)
+    final = pl.pallas_call(
+        functools.partial(final_kernel, n),
+        name="finish",
+        out_shape=outs,
+        in_specs=[smem()] + [vmem()] * 8,
+        out_specs=(vmem(),) * len(outs),
+        compiler_params=params(),
+    )(tie_map, x_own, y, dh, d_resid, vectors, f_sum, q_sum, small_sum)
+    grads = list(final[2:])
+    for index in (2, 5, 9):
+        grads[index] = turned(grads[index])
+    return (final[0][None], final[1][None]) + tuple(grads)
+
+
+def fits_grouped(mesh, block_input, span_place, qkv_weight):
+    width = qkv_weight.shape[1]
+    rows = block_input.shape[2] // mesh.shape["ctx"]
+    total = mesh.shape["ctx"] * mesh.shape["dp"]
+    return (
+        mesh.shape["ctx"] == 8
+        and block_input.shape[1] == 2
+        and HEADS % 4 == 0
+        and HEADS * HD == width
+        and rows % 16 == 0
+        and block_input.shape[2] % KCOLS == 0
+        and width % total == 0
+        and (width // total) % 8 == 0
+        and (width // 4) % (2 * (width // total)) == 0
+    )
+
+
 def solution(mesh):
-    placed = (
-        P("dp", None, "ctx", None),
-        P("dp", None, "ctx", None),
-        P(),
-        P("dp", None, None),
-        P("dp", None, None),
-        P(None, ("dp", "ctx")),
-        P(None, ("dp", "ctx")),
-        P(None, None, ("dp", "ctx")),
-        P(None, ("dp", "ctx")),
-        P(None, ("dp", "ctx")),
-        P(None, None, ("dp", "ctx")),
-        P(None, ("dp", "ctx")),
-        P(None, ("dp", "ctx")),
-        P(None, ("dp", "ctx")),
-        P(None, None, ("dp", "ctx")),
-        P(None, ("dp", "ctx")),
+    replicated_rows = P("dp", None, "ctx", None)
+    vector = P(None, ("dp", "ctx"))
+    columns = P(None, None, ("dp", "ctx"))
+    bank_specs = (
+        vector,
+        vector,
+        columns,
+        vector,
+        vector,
+        columns,
+        vector,
+        vector,
+        vector,
+        columns,
+        vector,
         P(None, ("dp", "ctx"), None),
-        P(None, ("dp", "ctx")),
-    )
-    return jax.shard_map(
-        on_device,
-        mesh=mesh,
-        in_specs=placed,
-        out_specs=(
-            P("dp", None, "ctx", None),
-            P("dp", None, "ctx", None),
-            P(None, ("dp", "ctx")),
-            P(None, ("dp", "ctx")),
-            P(None, None, ("dp", "ctx")),
-            P(None, ("dp", "ctx")),
-            P(None, ("dp", "ctx")),
-            P(None, None, ("dp", "ctx")),
-            P(None, ("dp", "ctx")),
-            P(None, ("dp", "ctx")),
-            P(None, ("dp", "ctx")),
-            P(None, None, ("dp", "ctx")),
-            P(None, ("dp", "ctx")),
-            P(None, ("dp", "ctx"), None),
-            P(None, ("dp", "ctx")),
-        ),
-        check_vma=False,
-    )
+        vector,
+    )
+
+    def step(*args):
+        if fits_grouped(mesh, args[0], args[4], args[7]):
+            plan = functools.partial(grouped_plan, mesh.shape["dp"])
+        else:
+            plan = general_plan
+        return jax.shard_map(
+            plan,
+            mesh=mesh,
+            in_specs=(
+                replicated_rows,
+                replicated_rows,
+                P(),
+                P("dp", None, None),
+                P("dp", None, None),
+            )
+            + bank_specs,
+            out_specs=(replicated_rows, replicated_rows) + bank_specs,
+            check_vma=False,
+        )(*args)
+
+    return step

time: 1190 us -> 202 us (0.17); the launches traced: 1170 us -> 202 us
  waiting for transfers between devices: 427 us -> 0 us
  matrix products: 249 us -> 0 us
  Pallas kernels: 0 us -> 201 us
  local copies, waits for them, and re-layouts: 165 us -> 0 us
  other arithmetic: 143 us -> 0 us
  blocking collectives: 116 us -> 0 us
  between operations: 41.4 us -> 0.82 us
  loops' own time: 27.3 us -> 0 us
    reduce_scatter x4 -> x0, waiting for transfers between devices: 322 us -> none  [the longest x1 140 us: on_device(): lax.psum_scatter(totals[11], ('dp', 'ctx'), scatter_dimension=0, tiled=True)]
    dot_general x150 -> x0, matrix products: 249 us -> none  [the longest x18 44.5 us: mutual(): jnp.einsum('hqk,qhd->khd', probs_other, gradout_heads, preferred_element_...]
    pallas_call x0 -> x2, Pallas kernels: none -> 201 us  [the longest x1 197 us: run_block(): pl.pallas_call(functools.partial(block_kernel, n, tuple(scratch)), name='...]
    all_gather x12 -> x0, waiting for transfers between devices: 103 us -> none  [the longest x1 49.3 us: on_device(): lax.all_gather(shards[11], ('dp', 'ctx'), axis=0, tiled=True)]
    dynamic_slice x130 -> x0, local copies, waits for them, and re-layouts: 101 us -> none  [the longest x126 97.9 us: over_blocks(): lax.scan(inner_step, state, (jnp.arange(piece_rows // block_rows, dtype=j...]
    unnamed x2 -> x0, blocking collectives: 79.9 us -> none
    reduce_sum x106 -> x0, other arithmetic: 76.8 us -> none  [the longest x38 28.8 us: segment_ids(): jnp.sum((positions[:, None] >= seq_ends[None, :]).astype(jnp.int32), axis=1)]
    and x54 -> x0, other arithmetic: 42.7 us -> none  [the longest x36 28.4 us: score_probs(): (query_seg[:, None] == key_seg[None, :]) & (key_pos[None, :] <= query_pos...]
  transfers between devices with their start and end apart: 16 -> 0, of which waited for: 7 -> 0; matrix products, arithmetic and copies ran while one was open for 46% -> 0% of each run, Pallas kernels for 0% -> 0%
where the time goes in v2:
time: 202 us
  Pallas kernels  201 us (100%)
    pallas_call x1, Pallas kernels, run_block(): pl.pallas_call(functools.partial(block_kernel, n, tuple(scratch)), name='...  197 us
    pallas_call x1, Pallas kernels, grouped_plan(): pl.pallas_call(functools.partial(final_kernel, n), name='finish', out_sha...  4.07 us

profile of v2, /device:TPU:23, one launch (start us, length us, event | category | flops | bytes accessed | tf_op | source)
XLA Modules:
  0.0 201.8 jit_solution(11464465263585785356)
XLA Ops:
  0.7 196.9 %block.1 = (bf16[2,144,768]{2,1,0:T(8,128)(2,1)}, f32[2,144,768]{2,1,0:T(8,128)}, f32[2,144,768]{2,1,0:T(8,128)}, f32[216,768]{1,0:T(8,128)}, f32[3,24,768]{2,1,...) custom-call(s32[13]{0:T(128)} %tie.3, s32[1,2,4]{2,1,0:T(2,128)} %lens.1, s32[1,2,8]{2,1,0:T(2,128)} %spans.1, ...), custom_call_target="tpu_custom_call" | custom-call | tf_op jit(solution)/shard_map/block/pallas_call | solution.py:1549
  197.6 4.1 %finish.1 = (bf16[2,144,768]{2,1,0:T(8,128)(2,1)}, bf16[2,144,768]{2,1,0:T(8,128)(2,1)}, f32[2,24]{1,0:T(2,128)}, f32[2,24]{1,0:T(2,128)}, f32[2,72,768]{2,1,0:T...) custom-call(s32[13]{0:T(128)} %tie.3, ...), custom_call_target="tpu_custom_call" | custom-call | tf_op jit(solution)/shard_map/finish/pallas_call | solution.py:1607

commit v3 on v2

--- a/solution.py
+++ b/solution.py
@@ -1024,15 +1024,12 @@
                 across(p, o, r, lane).wait_recv()
 
     gather_events = {
-        0: [lambda: line_event(1, (0,)), lambda: line_event(1, main)],
-        1: [lambda: line_event(2, (0,)), lambda: first_event(0, (0,))],
-        2: [lambda: line_event(3, (0,)), lambda: first_event(0, main)],
-        3: [lambda: line_event(2, main)],
-        4: [lambda: first_event(1, (0,)), lambda: first_event(1, main)],
-        5: [lambda: first_event(2, (0,))],
-        6: [lambda: line_event(3, main), lambda: first_event(3, (0,))],
-        7: [lambda: first_event(2, main)],
-        8: [lambda: first_event(3, main)],
+        0: [lambda: line_event(1, (0,)), lambda: first_event(0, (0,))],
+        1: [lambda: line_event(2, (0,)), lambda: line_event(3, (0,))],
+        2: [lambda: line_event(1, main)],
+        3: [lambda: first_event(1, (0,)), lambda: first_event(0, main)],
+        5: [lambda: first_event(2, (0,)), lambda: first_event(3, (0,))],
+        6: [lambda: first_event(1, main)],
     }
 
     def run_events(events, i):
@@ -1099,6 +1096,8 @@
             remote(stage.at[frm], target.at[frm], send.at[frm], recv.at[frm], z, frm).wait()
 
     exchange_start(s.stage, s.at_recv, s.s_asend, s.s_arecv)
+    for k in range(2, depth):
+        line_event(k, main)
     for k in range(depth):
         second_event(order(k), (0,))
     second_event(z, main)
@@ -1203,9 +1202,13 @@
         k, half = c // 2, c % 2
         o = order(k)
 
-        @pl.when((half == 0) & (k > 0))
-        def _():
-            second_event(o, main)
+        for kk in range(1, depth):
+
+            @pl.when((half == 0) & (k == kk))
+            def _(kk=kk):
+                if kk + 1 < depth:
+                    first_event(kk + 1, main)
+                second_event(order(kk), main)
 
         @pl.when(half == 0)
         def _():
@@ -1237,7 +1240,7 @@
         def _():
             start_sum(o, main)
 
-            @pl.when(k > 0)
+            @pl.when((k > 0) & (k < depth - 1))
             def _():
                 event_one(order(k - 1), main)
 
@@ -1268,6 +1271,7 @@
     s.vec_grad[5:6, :] = jnp.sum(d_h2 * unit_rows, axis=0, keepdims=True)
     s.vec_grad[6:7, :] = jnp.sum(d_h2, axis=0, keepdims=True)
     s.vec_grad[7:8, :] = jnp.sum(dy, axis=0, keepdims=True)
+    event_one(order(depth - 2), main)
     event_one(order(depth - 1), main)
     exchange_wait(s.stage, s.da_recv, s.s_dsend, s.s_drecv)
 

time: 202 us -> 191 us (0.946)
  Pallas kernels: 201 us -> 189 us
    pallas_call x1, Pallas kernels: 197 us -> 185 us  [run_block(): pl.pallas_call(functools.partial(block_kernel, n, tuple(scratch)), name='...]
where the time goes in v3:
time: 191 us; the launch traced here: 190 us
  Pallas kernels  189 us (99%)
    pallas_call x1, Pallas kernels, run_block(): pl.pallas_call(functools.partial(block_kernel, n, tuple(scratch)), name='...  185 us
    pallas_call x1, Pallas kernels, grouped_plan(): pl.pallas_call(functools.partial(final_kernel, n), name='finish', out_sha...  4.07 us

profile of v3, /device:TPU:23, one launch (start us, length us, event | category | flops | bytes accessed | tf_op | source)
XLA Modules:
  0.0 190.1 jit_solution(4497033986331256807)
XLA Ops:
  0.7 185.2 %block.1 = (bf16[2,144,768]{2,1,0:T(8,128)(2,1)}, f32[2,144,768]{2,1,0:T(8,128)}, f32[2,144,768]{2,1,0:T(8,128)}, f32[216,768]{1,0:T(8,128)}, f32[3,24,768]{2,1,...) custom-call(s32[13]{0:T(128)} %tie.3, s32[1,2,4]{2,1,0:T(2,128)} %lens.1, s32[1,2,8]{2,1,0:T(2,128)} %spans.1, ...), custom_call_target="tpu_custom_call" | custom-call | tf_op jit(solution)/shard_map/block/pallas_call | solution.py:1553
  185.8 4.1 %finish.1 = (bf16[2,144,768]{2,1,0:T(8,128)(2,1)}, bf16[2,144,768]{2,1,0:T(8,128)(2,1)}, f32[2,24]{1,0:T(2,128)}, f32[2,24]{1,0:T(2,128)}, f32[2,72,768]{2,1,0:T...) custom-call(s32[13]{0:T(128)} %tie.3, ...), custom_call_target="tpu_custom_call" | custom-call | tf_op jit(solution)/shard_map/finish/pallas_call | solution.py:1611

commit v4 on v3

--- a/solution.py
+++ b/solution.py
@@ -562,30 +562,31 @@
     return vectors, jnp.sum(jnp.where(keep, wide, 0.0), axis=0, keepdims=True)
 
 
-def gather_units(vectors, hidden_row, devices):
+def gather_vectors(vectors, devices):
     width = vectors.shape[1]
-    hidden_total = hidden_row.shape[1]
     unit = width // devices
-    per = hidden_total // devices
     tall = jnp.broadcast_to(vectors[None], (devices, SMALL, width)).reshape(devices * SMALL, width)
     row = iota((devices * SMALL, width), 0)
     col = iota((devices * SMALL, width), 1)
     tall = jnp.where(col // unit == row // SMALL, tall, 0.0).astype(BF)
     pick = (iota((width, 128), 0) % unit == iota((width, 128), 1)).astype(F32).astype(BF)
-    left = nn(tall, pick)
+    return nn(tall, pick).astype(BF).reshape(devices, SMALL, 128)
+
+
+def gather_hidden(hidden_row, devices):
+    hidden_total = hidden_row.shape[1]
+    per = hidden_total // devices
     wide = jnp.broadcast_to(hidden_row, (devices, hidden_total))
     keep = iota((devices, hidden_total), 1) // per == iota((devices, hidden_total), 0)
     wide = jnp.where(keep, wide, 0.0).astype(BF)
     pick = (iota((hidden_total, 128), 0) % per == iota((hidden_total, 128), 1)).astype(F32)
     firsts = nn(wide, pick.astype(BF)).astype(BF)
     chosen = (
-        iota((devices * SMALL, devices), 0) == iota((devices * SMALL, devices), 1) * SMALL
-    ).astype(F32).astype(BF)
-    right = nn(chosen, firsts)
-    return (
-        left.astype(BF).reshape(devices, SMALL, 128),
-        right.astype(BF).reshape(devices, SMALL, 128),
-    )
+        (iota((devices * SMALL, devices), 0) == iota((devices * SMALL, devices), 1) * SMALL)
+        .astype(F32)
+        .astype(BF)
+    )
+    return nn(chosen, firsts).astype(BF).reshape(devices, SMALL, 128)
 
 
 def group_slice(row, j, groups):
@@ -700,9 +701,9 @@
         "vec": vm((SMALL, w), F32),
         "hid": vm((halves, 1, chunk), F32),
         "hid_grad": vm((halves, 1, chunk), F32),
-        "stage": vm((8, rows, g)),
-        "at_recv": vm((8, rows, g)),
-        "da_recv": vm((8, rows, g)),
+        "stage": vm((8, rows + rows // 2, 128)),
+        "at_recv": vm((8, rows + rows // 2, 128)),
+        "da_recv": vm((8, rows + rows // 2, 128)),
         "resid": vm((both, w), F32),
         "unit2": vm((both, w), F32),
         "h2": vm((both, w)),
@@ -759,6 +760,18 @@
     }
 
 
+def fold(block):
+    half = block.shape[0] // 2
+    side = jnp.concatenate([block[:half, 128:], block[half:, 128:]], axis=1)
+    return jnp.concatenate([block[:, :128], side], axis=0)
+
+
+def unfold(tall):
+    rows = tall.shape[0] * 2 // 3
+    side = jnp.concatenate([tall[rows:, :64], tall[rows:, 64:]], axis=0)
+    return jnp.concatenate([tall[:rows], side], axis=1)
+
+
 def add_into(target, source):
     target[...] = (target[...].astype(F32) + source[...].astype(F32)).astype(BF)
 
@@ -1082,7 +1095,7 @@
 
     for e in range(8):
         at = pl.ds(spans[0, micro, e] * rows, rows)
-        s.stage[e] = s.o[at, 0:group].astype(BF)
+        s.stage[e] = fold(s.o[at, 0:group].astype(BF))
 
     def exchange_start(stage, target, send, recv):
         for k in range(1, 8):
@@ -1108,7 +1121,7 @@
     full = 2 * rows
     def attended():
         pieces = [
-            jnp.concatenate([s.at_recv[2 * g], s.at_recv[2 * g + 1]], axis=0)
+            jnp.concatenate([unfold(s.at_recv[2 * g]), unfold(s.at_recv[2 * g + 1])], axis=0)
             for g in range(groups)
         ]
         return jnp.concatenate(pieces, axis=1)
@@ -1240,7 +1253,7 @@
         def _():
             start_sum(o, main)
 
-            @pl.when((k > 0) & (k < depth - 1))
+            @pl.when(k > 0)
             def _():
                 event_one(order(k - 1), main)
 
@@ -1249,7 +1262,6 @@
     lax.fori_loop(0, 2 * depth, feed, 0)
 
     dy = g_down.astype(F32)
-    y_out[...] = s.resid[...].astype(BF).reshape(2, rows, width)
     d_h2 = dr_out[...].reshape(full, width)
     unit_rows = s.unit2[...]
     d_res = dy + norm_back(d_h2 * s.vec[5:6, :], unit_rows, s.scale2[...])
@@ -1258,10 +1270,11 @@
     d_attn = nn(g_mix, s.f_all[:, 0:unit, :].reshape(width, width)).astype(BF)
     for m in range(2):
         for g in range(groups):
-            s.stage[2 * g + m] = d_attn[
-                m * rows : (m + 1) * rows, g * group : (g + 1) * group
-            ]
+            s.stage[2 * g + m] = fold(
+                d_attn[m * rows : (m + 1) * rows, g * group : (g + 1) * group]
+            )
     exchange_start(s.stage, s.da_recv, s.s_dsend, s.s_drecv)
+    y_out[...] = s.resid[...].astype(BF).reshape(2, rows, width)
     out_grad = tn(g_mix, attended()).astype(BF).reshape(depth, 2, 2, 2, unit, width)
     s.gr[:, :, :, :, 0:unit, :] = out_grad
     for k in range(depth):
@@ -1271,12 +1284,13 @@
     s.vec_grad[5:6, :] = jnp.sum(d_h2 * unit_rows, axis=0, keepdims=True)
     s.vec_grad[6:7, :] = jnp.sum(d_h2, axis=0, keepdims=True)
     s.vec_grad[7:8, :] = jnp.sum(dy, axis=0, keepdims=True)
-    event_one(order(depth - 2), main)
     event_one(order(depth - 1), main)
+    hidden_row = jnp.concatenate([s.hid_grad[c] for c in range(2 * depth)], axis=1)
+    s.sg[:, :, 128:256] = gather_hidden(hidden_row, n.total)
     exchange_wait(s.stage, s.da_recv, s.s_dsend, s.s_drecv)
 
     for p in range(8):
-        s.da[p * rows : (p + 1) * rows, :] = s.da_recv[block_at(spans, micro, p, 8)]
+        s.da[p * rows : (p + 1) * rows, :] = unfold(s.da_recv[block_at(spans, micro, p, 8)])
     s.dk_acc[...] = jnp.zeros_like(s.dk_acc)
     s.dv_acc[...] = jnp.zeros_like(s.dv_acc)
 
@@ -1288,14 +1302,13 @@
         return go
 
     sum_events = {
-        0: [lambda: event_two(order(0), main)],
-        1: [lambda: event_two(order(1), main)],
-        2: [lambda: event_two(order(2), main), lambda: event_three(order(0), main)],
-        3: [out_events(event_one), lambda: event_three(order(1), main)],
-        4: [lambda: event_two(order(3), main)],
-        5: [out_events(event_two), lambda: event_three(order(2), main)],
-        6: [lambda: event_three(order(3), main)],
-        8: [out_events(event_three)],
+        0: [lambda: event_two(order(1), main)],
+        1: [lambda: event_two(order(2), main)],
+        3: [lambda: event_three(order(1), main), out_events(event_one)],
+        5: [lambda: event_two(order(3), main)],
+        6: [lambda: event_three(order(2), main), out_events(event_two)],
+        7: [lambda: event_two(order(0), main)],
+        8: [lambda: event_three(order(3), main), out_events(event_three), lambda: event_three(order(0), main)],
     }
 
     def query_block(i, carry):
@@ -1401,6 +1414,7 @@
     def dh_m():
         return remote(s.x_all.at[a, b, 1 - core], s.dh_mate, s.s_dhs.at[4], s.s_dhr.at[4], z, mate)
 
+
     def unsort(e, carry):
         late, kind, lane = e // 4, (e % 4) // 2, e % 2
         aa = jnp.where(kind == 0, jnp.where(late == 1, a, 1 - a), lane)
@@ -1432,10 +1446,7 @@
     s.vec_grad[0:2, :] = s.sums[0:2, :]
     s.vec_grad[2:3, :] = group_spread(query_bias, j, groups)
     s.vec_grad[3:4, :] = group_spread(value_bias, j, groups)
-    hidden_row = jnp.concatenate([s.hid_grad[c] for c in range(2 * depth)], axis=1)
-    left, right = gather_units(s.vec_grad[...], hidden_row, n.total)
-    s.sg[:, :, 0:128] = left
-    s.sg[:, :, 128:256] = right
+    s.sg[:, :, 0:128] = gather_vectors(s.vec_grad[...], n.total)
     to_all(lambda other: s.sg.at[other], s.s_sgs, s.s_sgr, s.sg_recv)
     s.sg_recv[me] = s.sg[me]
 
@@ -1632,6 +1643,7 @@
         and HEADS % 4 == 0
         and HEADS * HD == width
         and rows % 16 == 0
+        and width // 4 == 192
         and block_input.shape[2] % KCOLS == 0
         and width % total == 0
         and (width // total) % 8 == 0

time: 191 us -> 183 us (0.958)
  Pallas kernels: 189 us -> 181 us
    pallas_call x1, Pallas kernels: 185 us -> 177 us  [run_block(): pl.pallas_call(functools.partial(block_kernel, n, tuple(scratch)), name='...]
where the time goes in v4:
time: 183 us; the launch traced here: 181 us
  Pallas kernels  181 us (99%)
    pallas_call x1, Pallas kernels, run_block(): pl.pallas_call(functools.partial(block_kernel, n, tuple(scratch)), name='...  177 us
    pallas_call x1, Pallas kernels, grouped_plan(): pl.pallas_call(functools.partial(final_kernel, n), name='finish', out_sha...  4.07 us

profile of v4, /device:TPU:23, one launch (start us, length us, event | category | flops | bytes accessed | tf_op | source)
XLA Modules:
  0.0 181.5 jit_solution(13889848132577413735)
XLA Ops:
  0.7 176.6 %block.1 = (bf16[2,144,768]{2,1,0:T(8,128)(2,1)}, f32[2,144,768]{2,1,0:T(8,128)}, f32[2,144,768]{2,1,0:T(8,128)}, f32[216,768]{1,0:T(8,128)}, f32[3,24,768]{2,1,...) custom-call(s32[13]{0:T(128)} %tie.3, s32[1,2,4]{2,1,0:T(2,128)} %lens.1, s32[1,2,8]{2,1,0:T(2,128)} %spans.1, ...), custom_call_target="tpu_custom_call" | custom-call | tf_op jit(solution)/shard_map/block/pallas_call | solution.py:1564
  177.2 4.1 %finish.1 = (bf16[2,144,768]{2,1,0:T(8,128)(2,1)}, bf16[2,144,768]{2,1,0:T(8,128)(2,1)}, f32[2,24]{1,0:T(2,128)}, f32[2,24]{1,0:T(2,128)}, f32[2,72,768]{2,1,0:T...) custom-call(s32[13]{0:T(128)} %tie.3, ...), custom_call_target="tpu_custom_call" | custom-call | tf_op jit(solution)/shard_map/finish/pallas_call | solution.py:1622

commit v5 on v4

--- a/solution.py
+++ b/solution.py
@@ -667,7 +667,7 @@
         self.pack = 8 * rows
         self.packed = self.unit + 2 * self.per
         self.units = self.group // self.unit
-        cut = self.per - 8
+        cut = self.per
         self.parts = (
             (0, self.unit, "b"),
             (self.unit, cut, "b"),
@@ -1346,12 +1346,9 @@
     s.qkv[2] = s.dv_acc[...].astype(BF)
 
     pairs = n.units // 2
-    for kind in range(3):
-        s.gq[kind] = tn(s.qkv[kind], s.h[...]).astype(BF).reshape(pairs, 2, unit, width)
     q_mate = remote(
         s.gq.at[:, :, 1 - core], s.q_mate, s.s_gqc.at[0], s.s_gqc.at[1], z, mate
     )
-    q_mate.start()
 
     def q_route(kind, m):
         block = kind * n.total + j * n.units + m * 2 + core
@@ -1434,8 +1431,6 @@
         def _():
             dh_a1().start()
             dh_b1().start()
-            q_mate.wait_recv()
-            q_sums(q_send)
 
         return carry
 
@@ -1449,6 +1444,9 @@
     s.sg[:, :, 0:128] = gather_vectors(s.vec_grad[...], n.total)
     to_all(lambda other: s.sg.at[other], s.s_sgs, s.s_sgr, s.sg_recv)
     s.sg_recv[me] = s.sg[me]
+    for kind in range(3):
+        s.gq[kind] = tn(s.qkv[kind], s.h[...]).astype(BF).reshape(pairs, 2, unit, width)
+    q_mate.start()
 
     dh_a1().wait_recv()
     for e in range(2):
@@ -1458,6 +1456,8 @@
     for e in range(2):
         add_into(s.x_all.at[e, b, 1 - core], s.dh_b1.at[e])
     dh_b2().start()
+    q_mate.wait_recv()
+    q_sums(q_send)
     dh_b2().wait_recv()
     add_into(s.x_all.at[a, b, 1 - core], s.dh_b2)
     dh_m().start()

time: 183 us -> 181 us (0.989)
  Pallas kernels: 181 us -> 179 us
where the time goes in v5:
time: 181 us; the launch traced here: 180 us
  Pallas kernels  179 us (99%)
    pallas_call x1, Pallas kernels, run_block(): pl.pallas_call(functools.partial(block_kernel, n, tuple(scratch)), name='...  175 us
    pallas_call x1, Pallas kernels, grouped_plan(): pl.pallas_call(functools.partial(final_kernel, n), name='finish', out_sha...  4.07 us

profile of v5, /device:TPU:23, one launch (start us, length us, event | category | flops | bytes accessed | tf_op | source)
XLA Modules:
  0.0 180.2 jit_solution(11058510375641152276)
XLA Ops:
  0.7 175.3 %block.1 = (bf16[2,144,768]{2,1,0:T(8,128)(2,1)}, f32[2,144,768]{2,1,0:T(8,128)}, f32[2,144,768]{2,1,0:T(8,128)}, f32[216,768]{1,0:T(8,128)}, f32[3,24,768]{2,1,...) custom-call(s32[13]{0:T(128)} %tie.3, s32[1,2,4]{2,1,0:T(2,128)} %lens.1, s32[1,2,8]{2,1,0:T(2,128)} %spans.1, ...), custom_call_target="tpu_custom_call" | custom-call | tf_op jit(solution)/shard_map/block/pallas_call | solution.py:1564
  175.9 4.1 %finish.1 = (bf16[2,144,768]{2,1,0:T(8,128)(2,1)}, bf16[2,144,768]{2,1,0:T(8,128)(2,1)}, f32[2,24]{1,0:T(2,128)}, f32[2,24]{1,0:T(2,128)}, f32[2,72,768]{2,1,0:T...) custom-call(s32[13]{0:T(128)} %tie.3, ...), custom_call_target="tpu_custom_call" | custom-call | tf_op jit(solution)/shard_map/finish/pallas_call | solution.py:1622
